TPU v7x, 32 devices: a whole 2x2x4 slice. The times are simulated.
32 devices in a mesh: replica: 16 (over z, x, core), shard: 2 (over y).
Axes of the slice: x: 2, y: 2, z: 4, core: 2. Of those that a mesh axis runs over, the one named last changes fastest.
Arguments:
- frames: bfloat16 [32768, 768], P(('replica', 'shard')), may hold values from -6 to 6
- cotangent: bfloat16 [32768, 768], P(('replica', 'shard')), may hold values from -6 to 6
- segment_ids: int32 [32, 1024], P(('replica', 'shard')), may hold values from 0 to 7, never falling along the last dimension, each value on 1 to 512 neighbouring positions
- norm_gain: bfloat16 [2, 768], P(None, 'shard'), may hold values from 0.099609375 to 1.8984375
- norm_bias: bfloat16 [2, 768], P(None, 'shard'), may hold values from -2 to 2
- w_qkv: bfloat16 [768, 2304], P('shard'), may hold values from -0.21875 to 0.21875
- qv_bias: bfloat16 [2, 768], P(None, 'shard'), may hold values from -2 to 2
- w_out: bfloat16 [768, 768], P('shard'), may hold values from -0.875 to 0.875
- out_bias: bfloat16 [2, 768], P(None, 'shard'), may hold values from -2 to 2
- w_up: bfloat16 [768, 3072], P(None, 'shard'), may hold values from -0.21875 to 0.21875
- up_bias: bfloat16 [3072], P('shard'), may hold values from -3 to 3
- w_down: bfloat16 [3072, 768], P('shard'), may hold values from -0.109375 to 0.109375
Outputs:
- out_frames: bfloat16 [32768, 768], P(('replica', 'shard'))
- d_frames: float32 [32768, 768], P(('replica', 'shard'))
- d_norm_gain: float32 [2, 768], P(None, 'shard')
- d_norm_bias: float32 [2, 768], P(None, 'shard')
- d_w_qkv: float32 [768, 2304], P('shard')
- d_qv_bias: float32 [2, 768], P(None, 'shard')
- d_w_out: float32 [768, 768], P('shard')
- d_out_bias: float32 [2, 768], P(None, 'shard')
- d_w_up: float32 [768, 3072], P(None, 'shard')
- d_up_bias: float32 [3072], P('shard')
- d_w_down: float32 [3072, 768], P('shard')
Inputs may be any that keep to these rules, and one draw needn't show every extreme that they name: `segment_ids`: each row numbers the documents of one sequence in order: never falling, every number of 0 to 7 used, no document longer than 512 frames, and one exactly that long in every row.
All inputs are finite; a program needn't handle non-finite values.
Results may differ from a plain program's by a relative error of at most 0.018.
Values may be sent and summed in bfloat16 or wider, within the bound.
No kernel may reach another device: no remote copies, remote signals or barrier semaphores. Data moves between devices by JAX's collectives and lax.ppermute only.
A program may use at most 256 MiB of HBM per device.

v0:
```python
import functools
import math

import jax
import jax.numpy as jnp
from jax import lax
from jax.experimental import pallas as pl
from jax.experimental.pallas import tpu as pltpu
from jax.sharding import PartitionSpec as P

H = 12
EPS = 1e-05
NEG = -1e30
F32 = jnp.float32
BF = jnp.bfloat16
NN = (((1,), (0,)), ((), ()))
NT = (((1,), (1,)), ((), ()))
TN = (((0,), (0,)), ((), ()))
BLK = 256
GROUPS = 3
VM = pl.BlockSpec(memory_space=pltpu.VMEM)
SM = pl.BlockSpec(memory_space=pltpu.SMEM)
LIMIT = 14 << 20
ROWS = 512


def mm(a, b, dims=NN):
    return lax.dot_general(a, b, dims, preferred_element_type=F32)


def blocks(rows, body):
    for i in range(rows // ROWS):
        body(slice(i * ROWS, (i + 1) * ROWS))


def rows_of(i, size=BLK):
    return pl.ds(pl.multiple_of(i * size, size), size)


def call(kernel, name, outs, n_in, smem, scratch=(), flops=0, moved=0, far=(), fetch=(), limit=LIMIT, cost=4.0):
    outs = outs if isinstance(outs, tuple) else (outs,)
    fetch = dict(fetch)
    n_out = len(outs)
    scratch = list(scratch)
    n_scratch = len(scratch)
    manual = [outs[i] for i in far] + list(fetch.values())

    def body(*refs):
        ins, rest = list(refs[:n_in]), list(refs[n_in:])
        targets, rest = rest[:n_out], rest[n_out:]
        own, rest = rest[:n_scratch], rest[n_scratch:]
        sem, buffers = rest[-1], rest[:-1]
        reads, writes = {}, {}
        for j, i in enumerate(fetch):
            buffer = buffers[len(far) + j]
            reads[i] = pltpu.make_async_copy(ins[i], buffer, sem.at[len(far) + j])
            reads[i].start()
            ins[i] = buffer
        local_outs = list(targets)
        for j, i in enumerate(far):
            local_outs[i] = buffers[j]

        def done(i):
            writes[i] = pltpu.make_async_copy(buffers[far.index(i)], targets[i], sem.at[far.index(i)])
            writes[i].start()

        def need(i):
            if i in reads:
                reads.pop(i).wait()

        kernel(done, need, *ins, *local_outs, *own)
        for i in far:
            if i not in writes:
                done(i)
        for i in list(reads):
            need(i)
        for copy in writes.values():
            copy.wait()

    hbm = pl.BlockSpec(memory_space=pltpu.HBM)
    out = pl.pallas_call(
        body if manual else functools.partial(kernel, None, None),
        name=name,
        out_shape=tuple(pltpu.HBM(o.shape, o.dtype) if i in far else o for i, o in enumerate(outs)),
        in_specs=[hbm if i in fetch else SM if i < smem else VM for i in range(n_in)],
        out_specs=tuple(hbm if i in far else VM for i in range(n_out)),
        scratch_shapes=scratch + ([pltpu.VMEM(m.shape, m.dtype) for m in manual] + [pltpu.SemaphoreType.DMA((len(manual),))] if manual else []),
        compiler_params=pltpu.CompilerParams(vmem_limit_bytes=limit),
        cost_estimate=pl.CostEstimate(flops=int(flops * cost), bytes_accessed=int(moved * cost), transcendentals=0),
    )
    return out


def array(shape, dtype=BF):
    return jax.ShapeDtypeStruct(shape, dtype)


def standardize(values):
    centered = values - jnp.mean(values, axis=1, keepdims=True)
    inverse = lax.rsqrt(jnp.mean(centered * centered, axis=1, keepdims=True) + EPS)
    return centered * inverse, inverse


def enter_kernel(group, done, need, pos_ref, frames_ref, cot_ref, small_ref, far_ref, normed_ref, normedT_ref, sum_ref, whole_ref, *bias_refs):
    shard = pos_ref[0]
    size = small_ref.shape[1]
    shards = far_ref.shape[0] + 1
    for j in range(shards):
        value = jnp.where(shard == j, small_ref[...].astype(F32), 0.0)
        for k in range(1, shards):
            value = jnp.where(jnp.bitwise_xor(shard, k) == j, far_ref[k - 1].astype(F32), value)
        whole_ref[:, j * size : (j + 1) * size] = value
    for g, ref in enumerate(bias_refs):
        cols = slice(g * group, (g + 1) * group)
        ref[:, 0:group] = whole_ref[4:5, cols]
        ref[:, group : 2 * group] = jnp.zeros((1, group), F32)
        ref[:, 2 * group : 3 * group] = whole_ref[5:6, cols]
    sum_ref[...] = jnp.zeros_like(sum_ref)

    def step(at):
        unit, _inv = standardize(frames_ref[at, :].astype(F32))
        normed = (unit * whole_ref[0:1, :] + whole_ref[2:3, :]).astype(BF)
        normed_ref[at, :] = normed
        normedT_ref[:, at] = normed.T
        sum_ref[...] += jnp.sum(cot_ref[at, :].astype(F32), axis=0, keepdims=True)

    blocks(frames_ref.shape[0], step)


def enter(pos, frames, cot, small, far):
    rows, width = frames.shape
    group = width // GROUPS
    outs = (array((rows, width)), array((width, rows)), array((1, width), F32), array((8, width), F32))
    return call(
        functools.partial(enter_kernel, group), "enter", outs + (array((1, 3 * group), F32),) * GROUPS, 5, 1,
        flops=rows * width * 20, moved=rows * width * 8, far=(1,),
    )(pos, frames, cot, small, far)


def pack_kernel(group, done, need, pos_ref, w_ref, *outs):
    half = w_ref.shape[0] // 2
    d = group * GROUPS
    at = pl.ds(pl.multiple_of(pos_ref[1] * half, half), half)
    for g in range(GROUPS):
        for t in range(3):
            cols = slice(t * d + g * group, t * d + (g + 1) * group)
            to = slice(t * group, (t + 1) * group)
            outs[g][:, to] = w_ref[at, cols]
            outs[GROUPS + g][:, to] = w_ref[:, cols]


def pack(pos, w):
    rows, cols = w.shape
    group = cols // 3 // GROUPS
    return call(
        functools.partial(pack_kernel, group), "pack",
        (array((rows // 2, 3 * group)),) * GROUPS + (array((rows, 3 * group)),) * GROUPS, 2, 1, moved=rows * cols * 5,
    )(pos, w)


def pack_more_kernel(done, need, pos_ref, out_ref, up_ref, down_ref, half_ref, *outs):
    core = pos_ref[1]
    half = half_ref.shape[0]
    half_ref[...] = out_ref[pl.ds(pl.multiple_of(core * half, half), half), :]
    chunks = len(outs) // 2
    up_rows, down_rows = up_ref.shape[0] // 2, down_ref.shape[0] // chunks // 2
    chunk = 2 * down_rows
    for i in range(chunks):
        at = pl.ds(pl.multiple_of(core * up_rows, up_rows), up_rows)
        outs[2 * i][...] = up_ref[at, i * chunk : (i + 1) * chunk]
        at = pl.ds(pl.multiple_of(i * chunk + core * down_rows, down_rows), down_rows)
        outs[2 * i + 1][...] = down_ref[at, :]


def pack_more(pos, w_out, w_up, w_down, chunks):
    d, hid = w_up.shape
    chunk = hid // chunks
    return call(
        pack_more_kernel, "pack_more",
        (array((w_out.shape[0] // 2, d)),) + (array((d // 2, chunk)), array((chunk // 2, d))) * chunks, 4, 1,
        moved=d * hid * 6,
    )(pos, w_out, w_up, w_down)


def windows(seg):
    length = seg.shape[1]
    first = seg[0, ::BLK]
    last = seg[0, BLK - 1 :: BLK]
    begin = jnp.sum((seg < first[:, None]).astype(jnp.int32), axis=1)
    end = jnp.sum((seg <= last[:, None]).astype(jnp.int32), axis=1)
    begin = begin // 16 * 16
    count = (end - begin + BLK - 1) // BLK
    begin = jnp.minimum(begin, length - count * BLK)
    return jnp.stack([begin, count]).astype(jnp.int32)


def by_head(block, dh):
    width = block.shape[1]
    lane = lax.broadcasted_iota(jnp.int32, (1, width), 1) // dh
    zero = jnp.zeros_like(block)
    return jnp.concatenate([jnp.where(lane == h, block, zero) for h in range(width // dh)], axis=0)


def place(full_ref, pos_ref, own_ref, near_ref, far_ref):
    shard, core = pos_ref[0], pos_ref[1]
    size = own_ref.shape[0]
    half = size // 2
    full_ref[pl.ds(pl.multiple_of(shard * size, half), size), :] = own_ref[...]
    for k in range(near_ref.shape[0]):
        base = jnp.bitwise_xor(shard, k + 1) * size
        full_ref[pl.ds(pl.multiple_of(base + core * half, half), half), :] = near_ref[k]
        full_ref[pl.ds(pl.multiple_of(base + (1 - core) * half, half), half), :] = far_ref[k]


def attn_fwd_kernel(dh, done, need, pos_ref, win_ref, normed_ref, own_ref, near_ref, far_ref, bias_ref, segr_ref, segc_ref,
                    w_ref, proj_ref, att_ref, attT_ref, lse_ref, acc_ref):
    width = att_ref.shape[1]
    heads = width // dh
    length = normed_ref.shape[0]
    place(w_ref, pos_ref, own_ref, near_ref, far_ref)

    def project(i, _):
        at = rows_of(i)
        proj_ref[at, :] = (mm(normed_ref[at, :], w_ref[...]) + bias_ref[...]).astype(BF)
        return 0

    lax.fori_loop(0, length // BLK, project, 0)
    done(0)
    done(1)

    def queries(step, _):
        at = rows_of(step)
        q = (proj_ref[at, 0:width].astype(F32) * (1.0 / math.sqrt(dh))).astype(BF)
        qall = by_head(q, dh)
        segq = jnp.concatenate([segr_ref[:, at]] * heads, axis=1)
        acc_ref[...] = jnp.zeros_like(acc_ref)
        start = win_ref[0, step]

        def tile(j, carry):
            m_old, mass = carry
            ks = pl.ds(pl.multiple_of(start + j * BLK, 16), BLK)
            vT = proj_ref[ks, 2 * width : 3 * width].T
            same = segc_ref[ks, :] == segq
            s = jnp.where(same, mm(proj_ref[ks, width : 2 * width], qall, NT), NEG)
            m_new = jnp.maximum(m_old, jnp.max(s, axis=0, keepdims=True))
            p = jnp.exp(s - m_new)
            alpha = jnp.exp(m_old - m_new)
            mass = mass * alpha + jnp.sum(p, axis=0, keepdims=True)
            pb = p.astype(BF)
            for h in range(heads):
                hs, cs = slice(h * dh, (h + 1) * dh), slice(h * BLK, (h + 1) * BLK)
                acc_ref[hs, :] = acc_ref[hs, :] * alpha[:, cs] + mm(vT[hs, :], pb[:, cs])
            return m_new, mass

        carry = (jnp.full((1, heads * BLK), NEG, F32), jnp.zeros((1, heads * BLK), F32))
        peak, mass = lax.fori_loop(0, win_ref[1, step], tile, carry)
        lse_ref[:, rows_of(step, heads * BLK)] = peak + jnp.log(mass)
        outs = []
        for h in range(heads):
            outs.append((acc_ref[h * dh : (h + 1) * dh, :] / mass[:, h * BLK : (h + 1) * BLK]).astype(BF))
        oT = jnp.concatenate(outs, axis=0)
        attT_ref[:, at] = oT
        att_ref[at, :] = oT.T
        return 0

    lax.fori_loop(0, length // BLK, queries, 0)


def attn_fwd(dh, pos, win, normed, own, near, far, bias, segr, segc):
    length, d = normed.shape
    width = own.shape[1] // 3
    heads = width // dh
    return call(
        functools.partial(attn_fwd_kernel, dh), "attn_fwd",
        (array((d, 3 * width)), array((length, 3 * width)), array((length, width)), array((width, length)),
         array((1, length * heads), F32)),
        9, 2, [pltpu.VMEM((width, BLK), F32)],
        flops=2 * length * d * 3 * width + 2 * length * length * 256 * heads,
        moved=length * (d + 6 * width) * 2, far=(0, 1, 3), cost=0.1,
    )(pos, win, normed, own, near, far, bias, segr, segc)


def split_rows(pos_ref, left_ref, right, keep_ref, send_ref, first):
    shard, core = pos_ref[0], pos_ref[1]
    half = left_ref.shape[0] // keep_ref.shape[0] // 2
    for k in range(keep_ref.shape[0]):
        base = jnp.bitwise_xor(shard, k) * (2 * half)
        for ref, part in ((keep_ref, core), (send_ref, 1 - core)):
            rs = pl.ds(pl.multiple_of(base + part * half, half), half)
            ref[k, first : first + half, :] = mm(left_ref[rs, :], right).astype(BF)


def attn_bwd_kernel(dh, extra, done, need, pos_ref, win_ref, proj_ref, att_ref, g_ref, lse_ref, segr_ref, segc_ref, nT_ref, *refs):
    if extra:
        more_keep_ref, more_send_ref = refs[:2]
        refs = refs[2:]
    dproj_ref, keep_ref, send_ref, sums_ref, dk_ref, dv_ref, dqT_ref = refs
    length, width = att_ref.shape
    heads = width // dh
    scale = 1.0 / math.sqrt(dh)
    dk_ref[...] = jnp.zeros_like(dk_ref)
    dv_ref[...] = jnp.zeros_like(dv_ref)
    row = lax.broadcasted_iota(jnp.int32, (8, width), 0)
    col = lax.broadcasted_iota(jnp.int32, (8, width), 1) // dh
    pick = jnp.where(row == col, 1.0, 0.0).astype(BF)

    def queries(step, _):
        at = rows_of(step)
        q = (proj_ref[at, 0:width].astype(F32) * scale).astype(BF)
        g = g_ref[at, :]
        qall = by_head(q, dh)
        gall = by_head(g, dh)
        og = att_ref[at, :].astype(F32) * g.astype(F32)
        high = og.astype(BF)
        low = (og - high.astype(F32)).astype(BF)
        delta = mm(pick, high, NT) + mm(pick, low, NT)
        delta = jnp.concatenate([delta[h : h + 1, :] for h in range(heads)], axis=1)
        lse = lse_ref[:, rows_of(step, heads * BLK)]
        segq = jnp.concatenate([segr_ref[:, at]] * heads, axis=1)
        dqT_ref[...] = jnp.zeros_like(dqT_ref)
        start = win_ref[0, step]

        def tile(j, _):
            ks = pl.ds(pl.multiple_of(start + j * BLK, 16), BLK)
            kt = proj_ref[ks, width : 2 * width]
            vt = proj_ref[ks, 2 * width : 3 * width]
            kT = kt.T
            same = segc_ref[ks, :] == segq
            p = jnp.where(same, jnp.exp(mm(kt, qall, NT) - lse), 0.0)
            ds = (p * (mm(vt, gall, NT) - delta)).astype(BF)
            dv_ref[ks, :] += mm(p.astype(BF), gall)
            dk_ref[ks, :] += mm(ds, qall)
            for h in range(heads):
                hs = slice(h * dh, (h + 1) * dh)
                dqT_ref[hs, :] += mm(kT[hs, :], ds[:, h * BLK : (h + 1) * BLK])
            return 0

        lax.fori_loop(0, win_ref[1, step], tile, 0)
        dproj_ref[at, 0:width] = (dqT_ref[...] * scale).astype(BF).T
        return 0

    lax.fori_loop(0, length // BLK, queries, 0)
    dproj_ref[:, width : 2 * width] = dk_ref[...].astype(BF)
    dproj_ref[:, 2 * width :] = dv_ref[...].astype(BF)
    sums_ref[...] = jnp.sum(dproj_ref[...].astype(F32), axis=0, keepdims=True)
    first = 0
    if extra:
        first = more_keep_ref.shape[1]
        keep_ref[:, 0:first, :] = more_keep_ref[...]
        send_ref[:, 0:first, :] = more_send_ref[...]
    done(0)
    split_rows(pos_ref, nT_ref, dproj_ref[...], keep_ref, send_ref, first)


def attn_bwd(dh, pos, win, shards, proj, att, g, lse, segr, segc, nT, extra=()):
    length, width = att.shape
    d = nT.shape[0]
    heads = width // dh
    half = d // shards // 2 + (extra[0].shape[1] if extra else 0)
    return call(
        functools.partial(attn_bwd_kernel, dh, bool(extra)), "attn_bwd",
        (array((length, 3 * width)), array((shards, half, 3 * width)), array((shards, half, 3 * width)), array((1, 3 * width), F32)),
        9 + len(extra), 2, [pltpu.VMEM((length, width), F32), pltpu.VMEM((length, width), F32), pltpu.VMEM((width, BLK), F32)],
        flops=2 * length * d * 3 * width + 5 * length * length * 256 * heads,
        moved=length * (d + 8 * width) * 2, far=(0,),
    )(pos, win, proj, att, g, lse, segr, segc, nT, *extra)


def middle_kernel(done, need, pos_ref, frames_ref, a0, a1, a2, own_ref, near_ref, far_ref, whole_ref,
                  w_ref, middle_ref, n_ref, nT_ref):
    place(w_ref, pos_ref, own_ref, near_ref, far_ref)
    width = a0.shape[1]

    def step(at):
        total = frames_ref[at, :].astype(F32) + whole_ref[6:7, :]
        for g, a in enumerate((a0, a1, a2)):
            total = total + mm(a[at, :], w_ref[g * width : (g + 1) * width, :])
        middle_ref[at, :] = total
        unit, _inv = standardize(total)
        normed = (unit * whole_ref[1:2, :] + whole_ref[3:4, :]).astype(BF)
        n_ref[at, :] = normed
        nT_ref[:, at] = normed.T

    blocks(frames_ref.shape[0], step)


def middle(pos, frames, atts, own, near, far, whole):
    rows, d = frames.shape
    return call(
        middle_kernel, "middle",
        (array((d, d)), array((rows, d), F32), array((rows, d)), array((d, rows))), 9, 1,
        flops=2 * rows * d * d, moved=rows * d * 12, far=(0, 1), cost=0.1,
    )(pos, frames, *atts, own, near, far, whole)


def ffn_kernel(own, apart, fresh, offset, done, need, pos_ref, n_ref, nT_ref, cot_ref, *refs):
    refs = list(refs)
    first, second = refs.pop(0), refs.pop(0)
    if apart:
        first, second = (first, second), (refs.pop(0), refs.pop(0))
    bias_ref = refs.pop(0)
    prev_ref = None if fresh else refs.pop(0)
    act_ref, keep_ref, send_ref, bsum_ref, gn_ref = refs[:5]
    core = pos_ref[1]
    if own:
        up_ref, down_ref = first, second
    else:
        down_ref, up_ref = refs[5], refs[6]
        for ref, t in ((up_ref, 0), (down_ref, 1)):
            size = ref.shape[0] // 2
            ref[pl.ds(pl.multiple_of(core * size, size), size), :] = first[t][...]
            ref[pl.ds(pl.multiple_of((1 - core) * size, size), size), :] = second[t][...]
    d = n_ref.shape[1]
    chunk = act_ref.shape[1]

    if not own:
        done(5)
    up = up_ref[:, offset : offset + chunk]
    down = down_ref[offset : offset + chunk, :]
    acts, ghs = [], []
    for i in range(n_ref.shape[0] // BLK):
        at = slice(i * BLK, (i + 1) * BLK)
        hidden = mm(n_ref[at, :], up) + bias_ref[...]
        grad = mm(cot_ref[at, :], down, NT)
        phi = 0.5 + 0.5 * lax.erf(hidden * (1.0 / math.sqrt(2.0)))
        bell = jnp.exp(hidden * hidden * -0.5) * (1.0 / math.sqrt(2.0 * math.pi))
        act = (hidden * phi).astype(BF)
        gh = (grad * (phi + hidden * bell)).astype(BF)
        act_ref[at, :] = act
        base = jnp.zeros((BLK, d), F32) if fresh else prev_ref[at, :]
        gn_ref[at, :] = base + mm(gh, up, NT)
        acts.append(act)
        ghs.append(gh)
    done(0)
    act = jnp.concatenate(acts, axis=0)
    gh = jnp.concatenate(ghs, axis=0)
    bsum_ref[...] = jnp.sum(gh.astype(F32), axis=0, keepdims=True)
    d_down = mm(act, cot_ref[...], TN).astype(BF)
    d_up = mm(nT_ref[...], gh).astype(BF)
    if d > chunk:
        d_up = jnp.concatenate([d_up[r * chunk : (r + 1) * chunk, :] for r in range(d // chunk)], axis=1)
    first = core == 0
    keep_ref[...] = jnp.where(first, d_down, d_up)
    send_ref[...] = jnp.where(first, d_up, d_down)


def ffn(own, offset, pos, n, nT, cot, first, second, bias, grad):
    rows, d = n.shape
    chunk = bias.shape[1]
    fresh = grad is None
    apart = isinstance(first, tuple)
    args = [pos, n, nT, cot, *(first + second if apart else (first, second)), bias] + ([] if fresh else [grad])
    outs = (array((rows, chunk)), array((chunk, d)), array((chunk, d)), array((1, chunk), F32), array((rows, d), F32))
    if not own:
        outs = outs + (array((chunk, d)),)
    return call(
        functools.partial(ffn_kernel, own, apart, fresh, offset), "ffn", outs,
        len(args), 1, [] if own else [pltpu.VMEM((d, chunk), BF)], flops=10 * rows * d * chunk,
        moved=rows * d * 20,
        far=(0,) if own else (0, 5), limit=20 << 20,
    )(*args)


def turn_kernel(done, need, pos_ref, gn_ref, middle_ref, cot_ref, whole_ref, w_ref, t0, t1, t2,
                gm_ref, g0, g1, g2, keep_ref, send_ref, sums_ref, branch_ref, mixT_ref):
    width = g0.shape[1]
    sums_ref[...] = jnp.zeros_like(sums_ref)
    for g, t in enumerate((t0, t1, t2)):
        mixT_ref[g * width : (g + 1) * width, :] = t[...]

    def step(at):
        gn = gn_ref[at, :]
        unit, inverse = standardize(middle_ref[at, :])
        e = gn * whole_ref[1:2, :]
        gm = cot_ref[at, :].astype(F32) + inverse * (
            e - jnp.mean(e, axis=1, keepdims=True) - unit * jnp.mean(e * unit, axis=1, keepdims=True)
        )
        gm_ref[at, :] = gm
        branch = gm.astype(BF)
        branch_ref[at, :] = branch
        sums_ref[0:1, :] += jnp.sum(gn * unit, axis=0, keepdims=True)
        sums_ref[1:2, :] += jnp.sum(gn, axis=0, keepdims=True)
        sums_ref[2:3, :] += jnp.sum(branch.astype(F32), axis=0, keepdims=True)
        for g, out in enumerate((g0, g1, g2)):
            out[at, :] = mm(branch, w_ref[g * width : (g + 1) * width, :], NT).astype(BF)

    blocks(gn_ref.shape[0], step)
    split_rows(pos_ref, mixT_ref, branch_ref[...], keep_ref, send_ref, 0)


def turn(pos, shards, gn, mid, cot, whole, w, attTs):
    rows, d = gn.shape
    width = d // GROUPS
    return call(
        turn_kernel, "turn",
        (array((rows, d), F32),) + (array((rows, width)),) * 3 + (array((shards, d // shards // 2, d)),) * 2 + (array((8, d), F32),),
        9, 1, [pltpu.VMEM((rows, d), BF), pltpu.VMEM((d, rows), BF)],
        flops=4 * rows * d * d, moved=rows * d * 20,
    )(pos, gn, mid, cot, whole, w, *attTs)


def leave_kernel(shards, ups, done, need, pos_ref, frames_ref, gm_ref, whole_ref, p0, p1, p2, w0, w1, w2, two_ref, cot_ref, *refs):
    qv_refs, up_refs, (out_ref, small_ref, tall_ref) = refs[:GROUPS], refs[GROUPS : GROUPS + ups], refs[GROUPS + ups :]
    tall_ref[...] = jnp.zeros_like(tall_ref)

    def step(at):
        gn = 0.0
        for i, (p, w) in enumerate(((p0, w0), (p1, w1), (p2, w2))):
            need(4 + i)
            need(7 + i)
            gn = gn + mm(p[at, :], w[...], NT)
        unit, inverse = standardize(frames_ref[at, :].astype(F32))
        e = gn * whole_ref[0:1, :]
        out_ref[at, :] = gm_ref[at, :] + inverse * (
            e - jnp.mean(e, axis=1, keepdims=True) - unit * jnp.mean(e * unit, axis=1, keepdims=True)
        )
        tall_ref[0:1, :] += jnp.sum(gn * unit, axis=0, keepdims=True)
        tall_ref[2:3, :] += jnp.sum(gn, axis=0, keepdims=True)

    blocks(frames_ref.shape[0], step)
    tall_ref[1:2, :] = two_ref[0:1, :]
    tall_ref[3:4, :] = two_ref[1:2, :]
    tall_ref[6:7, :] = two_ref[2:3, :]
    tall_ref[7:8, :] = cot_ref[...]
    for g, ref in enumerate(qv_refs):
        width = ref.shape[1] // 3
        cols = slice(g * width, (g + 1) * width)
        tall_ref[4:5, cols] = ref[:, 0:width]
        tall_ref[5:6, cols] = ref[:, 2 * width :]
    size = tall_ref.shape[1] // shards
    for k in range(shards):
        want = jnp.bitwise_xor(pos_ref[0], k)
        value = jnp.zeros((8, size), F32)
        for j in range(shards):
            value = jnp.where(want == j, tall_ref[:, j * size : (j + 1) * size], value)
        small_ref[k, 0:8, :] = value
        row = 8
        for ref in up_refs[k * ups // shards : (k + 1) * ups // shards]:
            for c in range(ref.shape[1] // size):
                small_ref[k, row : row + 1, :] = ref[:, c * size : (c + 1) * size]
                row += 1


def leave(pos, shards, frames, gm, whole, dprojs, ws, two, cot_sum, qvs, ups):
    rows, d = frames.shape
    return call(
        functools.partial(leave_kernel, shards, len(ups)), "leave",
        (array((rows, d), F32), array((shards, 12, d // shards), F32)), 12 + len(qvs) + len(ups), 1,
        [pltpu.VMEM((8, d), F32)], flops=6 * rows * d * d, moved=rows * d * 16, far=(0,),
        fetch={4 + i: array(v.shape) for i, v in enumerate((*dprojs, *ws))}, limit=30 << 20,
    )(pos, frames, gm, whole, *dprojs, *ws, two, cot_sum, *qvs, *ups)


def result_kernel(n, offsets, done, need, middle_ref, whole_ref, *refs):
    acts, downs, out_ref = refs[:n], refs[n : 2 * n], refs[2 * n]
    need(0)

    def step(at):
        total = middle_ref[at, :] + whole_ref[7:8, :]
        for i, (a, w, offset) in enumerate(zip(acts, downs, offsets)):
            need(2 + i)
            need(2 + n + i)
            total = total + mm(a[at, :], w[offset : offset + a.shape[1], :])
        out_ref[at, :] = total.astype(BF)

    blocks(middle_ref.shape[0], step)


def result(mid, whole, acts, downs, offsets):
    rows, d = mid.shape
    n = len(acts)
    fetch = {0: array(mid.shape, F32)}
    fetch.update({2 + i: array(v.shape) for i, v in enumerate((*acts, *downs))})
    return call(
        functools.partial(result_kernel, n, offsets), "result", array((rows, d)), 2 + 2 * n, 0,
        flops=2 * rows * d * n * acts[0].shape[1], moved=rows * d * 14, far=(0,), fetch=fetch, limit=36 << 20,
    )(mid, whole, *acts, *downs)


def swap(value, axis, size, bit):
    return lax.ppermute(value, axis, [(i, i ^ bit) for i in range(size)])


def after(value, *others):
    return lax.optimization_barrier((value, *others))[0]


def total(terms):
    out = terms[0].astype(F32)
    for t in terms[1:]:
        out = out + t.astype(F32)
    return out.astype(terms[0].dtype)


def bits_of(size):
    return [1 << b for b in range(size.bit_length() - 1)]


def spread(own, shards):
    stack = own[None]
    for bit in bits_of(shards):
        stack = jnp.concatenate([stack, swap(stack, "shard", shards, bit)], axis=0)
    return stack


def others(own, shards):
    return swap(own, "shard", 2, 1)[None] if shards == 2 else spread(own, shards)[1:]


class Order:
    def __init__(self):
        self.token = None
        self.pins = []

    def land(self, *values):
        if self.token is not None:
            values = lax.optimization_barrier((*values, self.token))[:-1]
        self.pins += values
        return values[0] if len(values) == 1 else values

    def hold(self, *values):
        self.pins += values
        return values[0] if len(values) == 1 else values

    def run(self, kernel, value, token):
        if self.pins or self.token is not None:
            value = after(value, *self.pins, *([] if self.token is None else [self.token]))
        self.pins = []
        out = kernel(value)
        self.token = out[token]
        return out


def combine_kernel(groups, done, need, flag_ref, *refs):
    outs = list(refs[sum(len(terms) for terms, _ in groups) :])
    at = 0
    for terms, cut in groups:
        ins = refs[at : at + len(terms)]
        at += len(terms)

        def summed(rs):
            out = 0.0
            for ref, lead in zip(ins, terms):
                out = out + (ref[rs, :] if lead is None else ref[lead, rs, :]).astype(F32)
            return out

        if cut:
            send, keep = outs.pop(0), outs.pop(0)
            rows = send.shape[0]
            for ref, half in ((send, 1 - flag_ref[0]), (keep, flag_ref[0])):
                ref[...] = summed(pl.ds(pl.multiple_of(half * rows, rows), rows)).astype(ref.dtype)
        else:
            out = outs.pop(0)
            out[...] = summed(slice(None)).astype(out.dtype)


def combine(flag, groups):
    terms, spec, outs = [], [], []
    for group, cut in groups:
        group = [t if isinstance(t, tuple) else (t, None) for t in group]
        terms += [t for t, _ in group]
        spec.append(([lead for _, lead in group], cut))
        rows, cols = group[0][0].shape[-2:]
        outs += [array((rows // 2, cols), group[0][0].dtype)] * 2 if cut else [array((rows, cols), group[0][0].dtype)]
    return call(
        functools.partial(combine_kernel, spec), "combine", tuple(outs), 1 + len(terms), 1, flops=1000, limit=6 << 20,
    )(flag, *terms)


def join_kernel(done, need, flag_ref, part_ref, other_ref, out_ref):
    rows = part_ref.shape[0]
    for ref, half in ((part_ref, flag_ref[0]), (other_ref, 1 - flag_ref[0])):
        out_ref[pl.ds(pl.multiple_of(half * rows, rows), rows), :] = ref[...]


def join(flag, part, other):
    rows, cols = part.shape
    return call(join_kernel, "join", array((2 * rows, cols), part.dtype), 3, 1, flops=1000, limit=6 << 20)(flag, part, other)[0]


class Ring:
    def __init__(self, shards, replicas, order):
        self.shards, self.replicas, self.order = shards, replicas, order
        self.bits = bits_of(replicas)[1:]
        replica = lax.axis_index("replica")
        self.flags = {bit: ((replica // bit) % 2).astype(jnp.int32)[None] for bit in bits_of(replicas)}

    def swap(self, value, bit):
        return swap(value, "replica", self.replicas, bit)

    def total(self, terms):
        return combine(self.flags[1], [(terms, False)])[0] if len(terms) > 1 else terms[0]

    def to_shard(self, pieces):
        for bit in reversed(bits_of(self.shards)):
            if bit == 1:
                send = self.order.hold(self.total(pieces[1]))
                return pieces[0], swap(send, "shard", self.shards, bit)
            send = self.order.hold(jnp.stack([self.total(p) for p in pieces[bit:]]))
            got = swap(send, "shard", self.shards, bit)
            pieces = [p + [(got, k)] for k, p in enumerate(pieces[:bit])]

    def to_halves(self, chunks, bit):
        outs = combine(self.flags[bit], [(terms, True) for terms in chunks])
        self.order.hold(*outs)
        return [([outs[2 * i + 1]], self.swap(outs[2 * i], bit)) for i in range(len(chunks))]

    def to_half(self, terms, bit):
        return self.to_halves([terms], bit)[0]

    def whole(self, part, bit):
        return join(self.flags[bit], part, self.swap(part, bit))

    def both(self, part, bit):
        return self.total([part, self.swap(part, bit)])


def local(replicas, shards, frames, cotangent, segment_ids, norm_gain, norm_bias, w_qkv, qv_bias, w_out, out_bias,
          w_up, up_bias, w_down):
    rows, d = frames.shape
    dh = d // H
    group = d // GROUPS
    hid = up_bias.shape[0]
    chunks = max(1, hid // d)
    chunk = hid // chunks
    shard = lax.axis_index("shard")
    core = lax.axis_index("replica") % 2
    pos = jnp.stack([shard, core]).astype(jnp.int32)
    order = Order()
    ring = Ring(shards, replicas, order)
    run, land, hold = order.run, order.land, order.hold
    twin = lambda v: ring.swap(v, 1)
    win = windows(segment_ids)
    segc = segment_ids.reshape(rows, 1)
    bias_own = up_bias.reshape(1, hid)

    small = jnp.concatenate([norm_gain, norm_bias, qv_bias, out_bias], axis=0)
    small_far = others(small, shards)
    packed = run(lambda v: pack(pos, v), w_qkv, 0)
    qkv_own = packed[GROUPS:]
    near = [others(packed[0], shards)]
    bias_far = others(bias_own, shards)
    more = run(lambda v: pack_more(pos, v, w_up, w_down, chunks), w_out, 0)
    pairs = [(more[1 + 2 * i], more[2 + 2 * i]) for i in range(chunks)]
    if chunk == d:
        pairs = [(jnp.stack(p),) for p in pairs]
    small_far = land(small_far)
    bias_far = land(bias_far)
    normed, normedT, cot_sum, whole, *qv = run(lambda v: enter(pos, v, cotangent, small, small_far), frames, 2)
    near[0] = land(near[0])
    far = [land(twin(near[0]))]
    near += [others(after(packed[g], near[0]), shards) for g in range(1, GROUPS)]

    ws, projs, atts, attTs, lses = [], [], [], [], []
    for g in range(GROUPS):
        w, proj, att, attT, lse = run(
            lambda v: attn_fwd(dh, pos, win, v, qkv_own[g], near[g], far[g], qv[g], segment_ids, segc), normed, 4)
        ws.append(w)
        projs.append(proj)
        atts.append(att)
        attTs.append(attT)
        lses.append(lse)
        if g == 0:
            near[1:] = land(*near[1:])
            far += land(*[twin(v) for v in near[1:]])
            near_out = others(after(more[0], near[1]), shards)
            fetched = [[others(after(v, *far[1:]), shards) for v in pairs[0]]]
        if g == 1:
            fetched += [[others(after(v, lse), shards) for v in pairs[i]] for i in range(1, chunks)]
    near_out = land(near_out)
    far_out = land(twin(near_out))
    w_out_all, mid, n_two, nT_two = run(lambda v: middle(pos, v, atts, w_out, near_out, far_out, whole), frames, 3)

    grad, acts, downs, offsets, up_sums = None, [], [], [], []
    pieces = [[None] * shards for _ in range(chunks)]
    waiting, pending = [], []
    chains, got = [None] * chunks, [None] * chunks
    x = ring.bits[0]
    brought = [None] * chunks
    for k in range(shards):
        for i in range(chunks):
            bias = (bias_own if k == 0 else bias_far[k - 1])[:, i * chunk : (i + 1) * chunk].astype(F32)
            if k == 0:
                out = run(lambda v: ffn(True, i * chunk, pos, v, nT_two, cotangent, w_up, w_down, bias, grad), n_two, 3)
                downs.append(w_down)
                offsets.append(i * chunk)
            else:
                if brought[i] is None:
                    a = [land(v) for v in fetched[i]]
                    brought[i] = a, [land(twin(v)) for v in a]
                elif late[0] is not None:
                    brought[0] = brought[0][0], [land(v) for v in late[0]]
                    late[0] = None
                a, b = [tuple(v[k - 1] for v in half) for half in brought[i]]
                a, b = (a[0], b[0]) if len(a) == 1 else (a, b)
                out = run(lambda v: ffn(False, 0, pos, v, nT_two, cotangent, a, b, bias, grad), n_two, 3)
                downs.append(out[5])
                offsets.append(0)
            if k == 0 and i == 0:
                a = [land(v) for v in fetched[0]]
                late = [[twin(v) for v in a]]
                brought[0] = a, None
            acts.append(out[0])
            up_sums.append(out[3])
            grad = out[4]
            last = k == shards - 1
            if k == 0 and shards == 2:
                pieces[i][k] = [out[1]]
                waiting.append((i, out[2]))
            elif last and i == chunks - 1 and i % 2:
                pieces[i][k] = [out[1]]
                final = twin(hold(out[2]))
                for j, other in pending:
                    pieces[j][0].append(land(other))
                pending = []
                continue
            else:
                pieces[i][k] = [out[1], land(twin(out[2]))]
                early = [(j, twin(after(send, pieces[i][k][1]))) for j, send in waiting]
                for j, other in pending:
                    pieces[j][0].append(land(other))
                waiting, pending = [], early
            if last:
                if i % 2 == 0:
                    chains[i], got[i] = ring.to_shard(pieces[i])
                else:
                    chains[i] = ring.to_halves(pieces[i], x)

    out = run(lambda v: turn(pos, shards, v, mid, cotangent, whole, w_out_all, attTs), grad, 6)
    gm, gs, out_keep, out_send, sums_two = out[0], out[1:4], out[4], out[5], out[6]
    if chunks % 2 == 0:
        pieces[-1][-1].append(land(final))
        chains[-1] = ring.to_halves(pieces[-1], x)
    dprojs, qv_sums, attn = [], [], []

    def back(g, extra=(), go=True):
        dproj, keep, send, sums = run(
            lambda v: attn_bwd(dh, pos, win, shards, projs[g], atts[g], v, lses[g], segment_ids, segc, normedT, extra), gs[g], 3)
        dprojs.append(dproj)
        qv_sums.append(sums)
        return keep, twin(hold(send)) if go else send

    def meet(keep, other):
        other = land(other)
        return ring.to_shard([[(keep, k), (other, k)] for k in range(shards)])

    z, far_bit, *last_bits = ring.bits[1:]
    even, odd = range(0, chunks, 2), range(1, chunks, 2)
    one = back(0, (out_keep, out_send))
    for i in even:
        chains[i], got[i] = ring.to_half(chains[i] + [land(got[i])], x)
    keep, send = back(1, (), False)
    for i in odd:
        chains[i], got[i] = ring.to_shard([keep_ + [land(v)] for keep_, v in chains[i]])
    one, one_got = meet(*one)
    two = back(2, (keep, send))
    for i in (*even, *odd):
        chains[i], got[i] = ring.to_half(chains[i] + [land(got[i])], z)
    d_frames, small_grads = run(
        lambda v: leave(pos, shards, frames, v, whole, dprojs, ws, sums_two, cot_sum, qv_sums, up_sums), gm, 1)
    two, two_got = meet(*two)
    one, one_got = ring.to_half(one + [land(one_got)], x)
    for i in range(chunks):
        chains[i] = hold(ring.total(chains[i] + [land(got[i])]))
        got[i] = ring.swap(chains[i], far_bit)
        order.token = chains[i]
    small, small_got = ring.to_shard([[small_grads[k]] for k in range(shards)])
    small = hold(ring.total(small + [land(small_got)]))
    small_got = ring.swap(small, x)
    out_frames, = run(lambda v: result(v, whole, acts, downs, tuple(offsets)), mid, 0)

    def add_step(part, other):
        order.token = ring.total([*part, after(other, order.token)])
        return order.token

    def join_step(part, other, bit):
        order.token = join(ring.flags[bit], part, after(other, order.token))
        return order.token

    full, wait = [None] * chunks, [None] * chunks

    def add_far(i):
        full[i] = add_step([chains[i]], got[i])
        for bit in last_bits:
            full[i] = add_step([full[i]], ring.swap(full[i], bit))
        wait[i] = ring.swap(full[i], z)

    def join_next(i, bit, next_bit):
        full[i] = join_step(full[i], wait[i], bit)
        wait[i] = ring.swap(full[i], next_bit)

    tail = range(1, chunks)
    small = add_step([small], small_got)
    small_got = ring.swap(small, z)
    add_far(0)
    one = add_step(one, one_got)
    one_got = ring.swap(one, z)
    send, keep = combine(ring.flags[x], [([*two, after(two_got, order.token)], True)])
    order.token = send
    two_got = ring.swap(send, x)
    for i in tail:
        add_far(i)
    join_next(0, z, x)
    small = add_step([small], small_got)
    small_got = ring.swap(small, 1)
    one = add_step([one], one_got)
    one_got = ring.swap(one, far_bit)
    small = add_step([small], small_got)
    small_got = ring.swap(small, far_bit)
    two = add_step([keep], two_got)
    two_got = ring.swap(two, z)
    for i in tail:
        join_next(i, z, x)
    two = add_step([two], two_got)
    two_got = ring.swap(two, far_bit)
    join_next(0, x, 1)
    one = add_step([one], one_got)
    small = add_step([small], small_got)
    for bit in last_bits:
        one = add_step([one], ring.swap(one, bit))
        small = add_step([small], ring.swap(small, bit))
    one_got = ring.swap(one, x)
    two = add_step([two], two_got)
    for bit in last_bits:
        two = add_step([two], ring.swap(two, bit))
    two_got = ring.swap(two, x)
    for i in tail:
        join_next(i, x, 1)
    one = join_step(one, one_got, x)
    two = join_step(two, two_got, x)
    vec = small
    ffn_grads = [
        (jnp.where(core == 0, mine, other), jnp.where(core == 0, other, mine)) for mine, other in zip(full, wait)]
    attn_grads = []
    for mine in (one, two):
        other = twin(mine)
        attn_grads.append((jnp.where(core == 0, mine, other), jnp.where(core == 0, other, mine)))

    d_down = jnp.concatenate([c[0] for c in ffn_grads], axis=0).astype(F32)
    ups = []
    for c in ffn_grads:
        up = c[1]
        ups.append(jnp.concatenate([up[:, r * chunk : (r + 1) * chunk] for r in range(d // chunk)], axis=0))
    d_up = jnp.concatenate(ups, axis=1).astype(F32)
    half = d // shards // 2
    d_wout = jnp.concatenate([v[:half] for v in attn_grads[0]]).astype(F32)
    groups = [[v[half:] for v in attn_grads[0]], [v[:half] for v in attn_grads[1]], [v[half:] for v in attn_grads[1]]]
    d_qkv = jnp.concatenate([
        jnp.concatenate([g[c][:, t * group : (t + 1) * group] for t in range(3) for g in groups], axis=1)
        for c in range(2)]).astype(F32)
    return (
        out_frames, d_frames, vec[0:2], vec[2:4], d_qkv, vec[4:6], d_wout, vec[6:8], d_up,
        vec[8:].reshape(hid), d_down,
    )


def solution(mesh):
    both = P(("replica", "shard"), None)
    wide, tall, flat = P(None, "shard"), P("shard", None), P("shard")
    return jax.shard_map(
        functools.partial(local, mesh.shape["replica"], mesh.shape["shard"]),
        mesh=mesh,
        in_specs=(both, both, both, wide, wide, tall, wide, tall, wide, wide, flat, tall),
        out_specs=(both, both, wide, wide, tall, wide, tall, wide, wide, flat, tall),
        check_vma=False,
    )
```

profile of v0, /device:TPU:0, one launch (start us, length us, event | category | flops | bytes accessed | tf_op | source)
XLA Modules:
  0.0 322.7 jit_solution(17416084053987033134)
XLA Ops:
  0.8 1.6 copy-done.8
  2.4 1.4 pack.1
  6.8 3.0 collective-permute-start
  10.0 2.1 collective-permute-start.1
  12.7 1.7 copy-done.3
  14.3 1.7 copy-done.5
  17.9 3.3 %enter.1 = (bf16[1024,768]{1,0:T(8,128)(2,1)S(1)}, bf16[768,1024]{1,0:T(8,128)(2,1)}, f32[1,768]{1,0:T(1,128)S(1)}, f32[8,768]{1,0:T(8,128)S(1)}, f32[1,768]{1,0...) custom-call(s32[2]{0:T(128)S(1)} %pad_add_fusion.1.pos_ref.refs_0_, bf16[1024,768]{1,0:T(8,128)(2,1)S(1)} %copy-done, ...), custom_call_target="tpu_custom_call" | custom-call | flops 62914560 | bytes 25165824 | tf_op jit(solution)/shard_map/enter/pallas_call | solution.py:134
  21.3 1.2 collective-permute-start.3
  23.5 9.8 %attn_fwd.3 = (bf16[768,768]{1,0:T(8,128)(2,1)}, bf16[1024,768]{1,0:T(8,128)(2,1)}, bf16[1024,256]{1,0:T(8,128)(2,1)S(1)}, bf16[256,1024]{1,0:T(8,128)(2,1)}, f32[1,4096]{1,0:T(1,128)S(1)}) custom-call(s32[2]{0:T(128)S(1)} %pad_add_fusion.1.pos_ref.refs_0_, s32[2,4]{1,0:T(2,128)S(1)} %pad_add_fusion.refs_1_, ...), custom_call_target="tpu_custom_call" | custom-call | flops 335544320 | bytes 471859 | tf_op jit(solution)/shard_map/attn_fwd/pallas_call | solution.py:273
  33.2 3.8 %collective-permute-done.4 = bf16[192,768]{1,0:T(8,128)(2,1)S(1)} collective-permute-done((bf16[192,768]{1,0:T(8,128)(2,1)S(1)}, bf16[192,768]{1,0:T(8,128)(2,1)S(1)}, u32[]{:S(2)}, u32[]{:S(2)}) %collective-permute-start.4) | collective-permute-done | bytes 294944 | tf_op jit(solution)/shard_map/ppermute | solution.py:581
  37.1 1.2 collective-permute-start.6
  38.6 1.2 collective-permute-done.8.refs_5_
  39.8 9.3 %attn_fwd.4 = (bf16[768,768]{1,0:T(8,128)(2,1)}, bf16[1024,768]{1,0:T(8,128)(2,1)}, bf16[1024,256]{1,0:T(8,128)(2,1)S(1)}, bf16[256,1024]{1,0:T(8,128)(2,1)}, f32[1,4096]{1,0:T(1,128)S(1)}) custom-call(s32[2]{0:T(128)S(1)} %pad_add_fusion.1.pos_ref.refs_0_, s32[2,4]{1,0:T(2,128)S(1)} %pad_add_fusion.refs_1_, ...), custom_call_target="tpu_custom_call" | custom-call | flops 335544320 | bytes 471859 | tf_op jit(solution)/shard_map/attn_fwd/pallas_call | solution.py:273
  49.1 9.3 %attn_fwd.5 = (bf16[768,768]{1,0:T(8,128)(2,1)}, bf16[1024,768]{1,0:T(8,128)(2,1)}, bf16[1024,256]{1,0:T(8,128)(2,1)S(1)}, bf16[256,1024]{1,0:T(8,128)(2,1)}, f32[1,4096]{1,0:T(1,128)S(1)}) custom-call(s32[2]{0:T(128)S(1)} %pad_add_fusion.1.pos_ref.refs_0_, s32[2,4]{1,0:T(2,128)S(1)} %pad_add_fusion.refs_1_, ...), custom_call_target="tpu_custom_call" | custom-call | flops 335544320 | bytes 471859 | tf_op jit(solution)/shard_map/attn_fwd/pallas_call | solution.py:273
  58.9 6.2 %collective-permute-start.10 = (bf16[2,384,768]{2,1,0:T(8,128)(2,1)S(1)}, bf16[2,384,768]{2,1,0:T(8,128)(2,1)S(1)}, u32[]{:S(2)}, u32[]{:S(2)}) collective-permute-start(bf16[2,384,768]{2,1,0:T(8,128)(2,1)S(1)} %pad_maximum_fusion), channel_id=1, source_target_pairs={{0,1},{1,0},{2,3},{3,2},{4,5},{5,4},{6,7},{7,6},{8,9},{9,8},{10,11... | collective-permute-start | bytes 3538952 | tf_op jit(solution)/shard_map/ppermute | solution.py:581
  65.2 4.0 %middle.1 = (bf16[768,768]{1,0:T(8,128)(2,1)}, f32[1024,768]{1,0:T(8,128)}, bf16[1024,768]{1,0:T(8,128)(2,1)S(1)}, bf16[768,1024]{1,0:T(8,128)(2,1)S(1)}) custom-call(s32[2]{0:T(128)S(1)} %pad_add_fusion.1.pos_ref.refs_0_, bf16[1024,768]{1,0:T(8,128)(2,1)S(1)} %copy-done, bf16[1024,256]{1,0:T(8,128)(2,1)S(1)} %get-tuple-element.210.refs_2_.refs_3_, ...), custom_call_target="tpu_custom_call" | custom-call | flops 120795952 | bytes 943718 | tf_op jit(solution)/shard_map/middle/pallas_call | solution.py:389
  69.2 8.2 %ffn.4 = (bf16[1024,768]{1,0:T(8,128)(2,1)}, bf16[768,768]{1,0:T(8,128)(2,1)S(1)}, bf16[768,768]{1,0:T(8,128)(2,1)}, f32[1,768]{1,0:T(1,128)S(1)}, f32[1024,768]{1,0:T(8,128)S(1)}) custom-call(s32[2]{0:T(128)S(1)} %pad_add_fusion.1.pos_ref.refs_0_, bf16[1024,768]{1,0:T(8,128)(2,1)S(1)} %get-tuple-element.239.refs_1_, ...), custom_call_target="tpu_custom_call" | custom-call | flops 24159191040 | bytes 62914560 | tf_op jit(solution)/shard_map/ffn/pallas_call | solution.py:456
  78.4 13.5 %collective-permute-done.10 = bf16[2,384,768]{2,1,0:T(8,128)(2,1)S(1)} collective-permute-done((bf16[2,384,768]{2,1,0:T(8,128)(2,1)S(1)}, bf16[2,384,768]{2,1,0:T(8,128)(2,1)S(1)}, u32[]{:S(2)}, u32[]{:S(2)}) %collective-permute-start.10) | collective-permute-done | bytes 1179680 | tf_op jit(solution)/shard_map/ppermute | solution.py:581
  91.9 8.7 %ffn.5 = (bf16[1024,768]{1,0:T(8,128)(2,1)}, bf16[768,768]{1,0:T(8,128)(2,1)S(1)}, bf16[768,768]{1,0:T(8,128)(2,1)}, f32[1,768]{1,0:T(1,128)S(1)}, f32[1024,768]{1,0:T(8,128)S(1)}) custom-call(s32[2]{0:T(128)S(1)} %pad_add_fusion.1.pos_ref.refs_0_, bf16[1024,768]{1,0:T(8,128)(2,1)S(1)} %get-tuple-element.239.refs_1_, ...), custom_call_target="tpu_custom_call" | custom-call | flops 24159191040 | bytes 62914560 | tf_op jit(solution)/shard_map/ffn/pallas_call | solution.py:456
  101.6 7.3 %ffn.6 = (bf16[1024,768]{1,0:T(8,128)(2,1)}, bf16[768,768]{1,0:T(8,128)(2,1)S(1)}, bf16[768,768]{1,0:T(8,128)(2,1)S(1)}, f32[1,768]{1,0:T(1,128)S(1)}, f32[1024,...) custom-call(s32[2]{0:T(128)S(1)} %pad_add_fusion.1.pos_ref.refs_0_, bf16[1024,768]{1,0:T(8,128)(2,1)S(1)} %get-tuple-element.239.refs_1_, ...), custom_call_target="tpu_custom_call" | custom-call | flops 24159191040 | bytes 62914560 | tf_op jit(solution)/shard_map/ffn/pallas_call | solution.py:456
  108.9 8.1 %collective-permute-done.13 = bf16[2,384,768]{2,1,0:T(8,128)(2,1)S(1)} collective-permute-done((bf16[2,384,768]{2,1,0:T(8,128)(2,1)S(1)}, bf16[2,384,768]{2,1,0:T(8,128)(2,1)S(1)}, u32[]{:S(2)}, u32[]{:S(2)}) %collective-permute-start.13) | collective-permute-done | bytes 1179680 | tf_op jit(solution)/shard_map/ppermute | solution.py:581
  117.5 2.3 collective-permute-done.14
  119.8 1.7 collective-permute-done.12.refs_1_
  122.4 8.7 %ffn.7 = (bf16[1024,768]{1,0:T(8,128)(2,1)}, bf16[768,768]{1,0:T(8,128)(2,1)S(1)}, bf16[768,768]{1,0:T(8,128)(2,1)}, f32[1,768]{1,0:T(1,128)S(1)}, f32[1024,768]{1,0:T(8,128)S(1)}, /*index=5*/bf16[768,768]{1,0:T(8,128)(2,1)}) custom-call(s32[2]{0:T(128)S(1)} %pad_add_fusion.1.pos_ref.refs_0_, bf16[1024,768]{1,0:T(8,128)(2,1)S(1)} %get-tuple-element.239.refs_1_, ...), custom_call_target="tpu_custom_call" | custom-call | flops 24159191040 | bytes 62914560 | tf_op jit(solution)/shard_map/ffn/pallas_call | solution.py:456
  131.1 1.1 copy-done.12
  132.2 1.7 copy-done.44
  134.0 1.8 collective-permute-start.19
  135.8 1.9 copy-done.27
  137.6 1.3 copy-done.36
  142.0 1.9 copy-done.45
  143.9 5.2 %turn.1 = (f32[1024,768]{1,0:T(8,128)S(1)}, bf16[1024,256]{1,0:T(8,128)(2,1)S(1)}, bf16[1024,256]{1,0:T(8,128)(2,1)S(1)}, bf16[1024,256]{1,0:T(8,128)(2,1)S(1)},...) custom-call(s32[2]{0:T(128)S(1)} %pad_add_fusion.1.pos_ref.refs_0_, ...), custom_call_target="tpu_custom_call" | custom-call | flops 9663676416 | bytes 62914560 | tf_op jit(solution)/shard_map/turn/pallas_call | solution.py:494
  149.2 2.3 combine.26
  152.4 1.1 collective-permute-start.20
  153.6 10.5 %attn_bwd.3 = (bf16[1024,768]{1,0:T(8,128)(2,1)}, bf16[2,384,768]{2,1,0:T(8,128)(2,1)S(1)}, bf16[2,384,768]{2,1,0:T(8,128)(2,1)S(1)}, f32[1,768]{1,0:T(1,128)S(1)}) custom-call(s32[2]{0:T(128)S(1)} %pad_add_fusion.1.pos_ref.refs_0_, s32[2,4]{1,0:T(2,128)S(1)} %pad_add_fusion.refs_1_, bf16[1024,768]{1,0:T(8,128)(2,1)S(1)} %copy-done.31, ...), custom_call_target="tpu_custom_call" | custom-call | flops 26306674688 | bytes 23068672 | tf_op jit(solution)/shard_map/attn_bwd/pallas_call | solution.py:360
  164.2 1.8 combine.27
  166.1 4.4 %collective-permute-start.23 = (bf16[384,768]{1,0:T(8,128)(2,1)S(1)}, bf16[384,768]{1,0:T(8,128)(2,1)S(1)}, u32[]{:S(2)}, u32[]{:S(2)}) collective-permute-start(bf16[384,768]{1,0:T(8,128)(2,1)S(1)} %get-tuple-element.276), channel_id=1, source_target_pairs={{0,4},{2,6},{4,0},{6,2},{8,12},{10,14},{12,8},{14,10},{16,20},{18,... | collective-permute-start | bytes 1769480 | tf_op jit(solution)/shard_map/ppermute | solution.py:581
  170.5 11.2 %attn_bwd.4 = (bf16[1024,768]{1,0:T(8,128)(2,1)}, bf16[2,192,768]{2,1,0:T(8,128)(2,1)S(1)}, bf16[2,192,768]{2,1,0:T(8,128)(2,1)S(1)}, f32[1,768]{1,0:T(1,128)S(1)}) custom-call(s32[2]{0:T(128)S(1)} %pad_add_fusion.1.pos_ref.refs_0_, s32[2,4]{1,0:T(2,128)S(1)} %pad_add_fusion.refs_1_, bf16[1024,768]{1,0:T(8,128)(2,1)S(1)} %copy-done.32, ...), custom_call_target="tpu_custom_call" | custom-call | flops 26306674688 | bytes 23068672 | tf_op jit(solution)/shard_map/attn_bwd/pallas_call | solution.py:360
  181.9 3.9 %collective-permute-start.24 = (bf16[384,768]{1,0:T(8,128)(2,1)S(1)}, bf16[384,768]{1,0:T(8,128)(2,1)S(1)}, u32[]{:S(2)}, u32[]{:S(2)}) collective-permute-start(bf16[384,768]{1,0:T(8,128)(2,1)S(1)} %combine.28), channel_id=1, source_target_pairs={{0,1},{1,0},{2,3},{3,2},{4,5},{5,4},{6,7},{7,6},{8,9},{9,8},{10,11... | collective-permute-start | bytes 1769480 | tf_op jit(solution)/shard_map/ppermute | solution.py:581
  187.3 10.5 %attn_bwd.5 = (bf16[1024,768]{1,0:T(8,128)(2,1)}, bf16[2,384,768]{2,1,0:T(8,128)(2,1)S(1)}, bf16[2,384,768]{2,1,0:T(8,128)(2,1)S(1)}, f32[1,768]{1,0:T(1,128)S(1)}) custom-call(s32[2]{0:T(128)S(1)} %pad_add_fusion.1.pos_ref.refs_0_, s32[2,4]{1,0:T(2,128)S(1)} %pad_add_fusion.refs_1_, bf16[1024,768]{1,0:T(8,128)(2,1)S(1)} %copy-done.30, ...), custom_call_target="tpu_custom_call" | custom-call | flops 26306674688 | bytes 23068672 | tf_op jit(solution)/shard_map/attn_bwd/pallas_call | solution.py:360
  197.9 2.1 collective-permute-done.24.refs_2_
  200.2 3.6 %collective-permute-start.27 = (bf16[192,768]{1,0:T(8,128)(2,1)S(1)}, bf16[192,768]{1,0:T(8,128)(2,1)S(1)}, u32[]{:S(2)}, u32[]{:S(2)}) collective-permute-start(bf16[192,768]{1,0:T(8,128)(2,1)S(1)} %get-tuple-element.294), channel_id=1, source_target_pairs={{0,8},{2,10},{4,12},{6,14},{8,0},{10,2},{12,4},{14,6},{16,24},{18,... | collective-permute-start | bytes 884744 | tf_op jit(solution)/shard_map/ppermute | solution.py:581
  204.2 1.4 copy-done.48
  205.6 11.2 %leave.1 = (f32[1024,768]{1,0:T(8,128)}, f32[2,12,384]{2,1,0:T(8,128)S(1)}) custom-call(s32[2]{0:T(128)S(1)} %pad_add_fusion.1.pos_ref.refs_0_, bf16[1024,768]{1,0:T(8,128)(2,1)S(1)} %copy-done.1, f32[1024,768]{1,0:T(8,128)S(1)} %get-tuple-element.296.refs_2_, f32[8,768]{1,0:T(8,128)S(1)} %get-tuple-element.213.refs_8_.whole_ref.refs_3_.refs_1_, ...), custom_call_target="tpu_custom_call" | custom-call | flops 14495514624 | bytes 50331648 | tf_op jit(solution)/shard_map/leave/pallas_call | solution.py:546
  218.0 2.5 collective-permute-start.31
  221.8 1.7 collective-permute-start.35
  223.6 1.1 collective-permute-start.34
  225.2 11.9 %result.1 = bf16[1024,768]{1,0:T(8,128)(2,1)} custom-call(f32[1024,768]{1,0:T(8,128)S(1)} %copy-done.28, f32[8,768]{1,0:T(8,128)S(1)} %get-tuple-element.213.refs_8_.whole_ref.refs_3_.refs_1_, bf16[1024,768]{1,0:T(8,128)(2,1)S(1)} %copy-done.49, bf16[1024,768]{1,0:T(8,128)(2,1)S(1)} %copy-done.50, bf16[1024,768]{1,0:T(8,128)(2,1)S(1)} %copy-done.51, ...), custom_call_target="tpu_custom_call" | custom-call | flops 19327352832 | bytes 44040192 | tf_op jit(solution)/shard_map/result/pallas_call | solution.py:574
  237.1 4.3 %collective-permute-done.31.refs_1_ = bf16[192,768]{1,0:T(8,128)(2,1)S(1)} collective-permute-done((bf16[192,768]{1,0:T(8,128)(2,1)S(1)}, bf16[192,768]{1,0:T(8,128)(2,1)S(1)}, u32[]{:S(2)}, u32[]{:S(2)}) %collective-permute-start.31) | collective-permute-done | bytes 294944 | tf_op jit(solution)/shard_map/ppermute | solution.py:581
  241.7 2.1 collective-permute-start.37
  244.3 2.5 collective-permute-done.33.refs_1_
  247.7 5.5 %collective-permute-done.32.other_ref = bf16[192,768]{1,0:T(8,128)(2,1)S(1)} collective-permute-done((bf16[192,768]{1,0:T(8,128)(2,1)S(1)}, bf16[192,768]{1,0:T(8,128)(2,1)S(1)}, u32[]{:S(2)}, u32[]{:S(2)}) %collective-permute-start.32) | collective-permute-done | bytes 294944 | tf_op jit(solution)/shard_map/ppermute | solution.py:581
  254.1 12.1 %collective-permute-done.30.refs_1_ = f32[12,384]{1,0:T(8,128)S(1)} collective-permute-done((f32[12,384]{1,0:T(8,128)S(1)}, f32[12,384]{1,0:T(8,128)S(1)}, u32[]{:S(2)}, u32[]{:S(2)}) %collective-permute-start.30) | collective-permute-done | bytes 18464 | tf_op jit(solution)/shard_map/ppermute | solution.py:581
  268.6 4.1 %collective-permute-start.39 = (bf16[192,768]{1,0:T(8,128)(2,1)S(1)}, bf16[192,768]{1,0:T(8,128)(2,1)S(1)}, u32[]{:S(2)}, u32[]{:S(2)}) collective-permute-start(bf16[192,768]{1,0:T(8,128)(2,1)S(1)} %combine.43.refs_0_), channel_id=1, source_target_pairs={{0,16},{2,18},{4,20},{6,22},{8,24},{10,26},{12,28},{14,30},{16,0},... | collective-permute-start | bytes 884744 | tf_op jit(solution)/shard_map/ppermute | solution.py:581
  272.7 9.4 %collective-permute-done.42.refs_1_ = bf16[192,768]{1,0:T(8,128)(2,1)S(1)} collective-permute-done((bf16[192,768]{1,0:T(8,128)(2,1)S(1)}, bf16[192,768]{1,0:T(8,128)(2,1)S(1)}, u32[]{:S(2)}, u32[]{:S(2)}) %collective-permute-start.42) | collective-permute-done | bytes 294944 | tf_op jit(solution)/shard_map/ppermute | solution.py:581
  282.3 10.7 %collective-permute-done.39.refs_1_ = bf16[192,768]{1,0:T(8,128)(2,1)S(1)} collective-permute-done((bf16[192,768]{1,0:T(8,128)(2,1)S(1)}, bf16[192,768]{1,0:T(8,128)(2,1)S(1)}, u32[]{:S(2)}, u32[]{:S(2)}) %collective-permute-start.39) | collective-permute-done | bytes 294944 | tf_op jit(solution)/shard_map/ppermute | solution.py:581
  293.1 1.4 collective-permute-start.44
  294.5 5.0 %collective-permute-done.38.refs_1_ = f32[12,384]{1,0:T(8,128)S(1)} collective-permute-done((f32[12,384]{1,0:T(8,128)S(1)}, f32[12,384]{1,0:T(8,128)S(1)}, u32[]{:S(2)}, u32[]{:S(2)}) %collective-permute-start.38) | collective-permute-done | bytes 18464 | tf_op jit(solution)/shard_map/ppermute | solution.py:581
  300.0 1.6 collective-permute-start.48
  303.3 6.2 %collective-permute-done.48.other_ref = bf16[192,768]{1,0:T(8,128)(2,1)} collective-permute-done((bf16[192,768]{1,0:T(8,128)(2,1)S(1)}, bf16[192,768]{1,0:T(8,128)(2,1)}, u32[]{:S(2)}, u32[]{:S(2)}) %collective-permute-start.48) | collective-permute-done | bytes 294944 | tf_op jit(solution)/shard_map/ppermute | solution.py:581
  310.6 1.1 broadcast_select_fusion.7
  313.3 2.0 maximum_convert_fusion.2
  315.3 1.4 broadcast_select_fusion.1
  316.9 2.5 maximum_convert_fusion.1
  319.5 2.8 maximum_convert_fusion
  (252 shorter events, 30.5 us)
Async XLA Ops:
  0.7 12.0 %copy-start.2 = (bf16[384,768]{1,0:T(8,128)(2,1)S(1)}, bf16[384,768]{1,0:T(8,128)(2,1)}, u32[]{:S(2)}) copy-start(bf16[384,768]{1,0:T(8,128)(2,1)} %refs_5_.3) | copy-start | bytes 1769476
  6.8 14.4 %collective-permute-start = (bf16[192,768]{1,0:T(8,128)(2,1)}, bf16[192,768]{1,0:T(8,128)(2,1)}, u32[]{:S(2)}, u32[]{:S(2)}) collective-permute-start(bf16[192,768]{1,0:T(8,128)(2,1)} %get-tuple-element.176), channel_id=1, source_target_pairs={{0,1},{1,0},{2,3},{3,2},{4,5},{5,4},{6,7},{7,6},{8,9},{9,8},{10,11... | collective-permute-start | bytes 884744 | tf_op jit(solution)/shard_map/ppermute | solution.py:581
  9.8 7.4 %collective-permute-start.2 = (bf16[1,1536]{1,0:T(2,128)(2,1)S(1)}, bf16[1,1536]{1,0:T(2,128)(2,1)S(1)}, u32[]{:S(2)}, u32[]{:S(2)}) collective-permute-start(bf16[1,1536]{1,0:T(2,128)(2,1)S(1)} %reshape.157), channel_id=1, source_target_pairs={{0,1},{1,0},{2,3},{3,2},{4,5},{5,4},{6,7},{7,6},{8,9},{9,8},{10,11... | collective-permute-start | bytes 9224 | tf_op jit(solution)/shard_map/ppermute | solution.py:581
  10.0 7.3 %collective-permute-start.1 = (bf16[8,384]{1,0:T(8,128)(2,1)S(1)}, bf16[8,384]{1,0:T(8,128)(2,1)S(1)}, u32[]{:S(2)}, u32[]{:S(2)}) collective-permute-start(bf16[8,384]{1,0:T(8,128)(2,1)S(1)} %pad_maximum_fusion.2.refs_3_), channel_id=1, source_target_pairs={{0,1},{1,0},{2,3},{3,2},{4,5},{5,4},{6,7},{7,6},{8,9},{9,8},{10,11... | collective-permute-start | bytes 18440 | tf_op jit(solution)/shard_map/ppermute | solution.py:581
  21.2 2.2 collective-permute-start.5
  21.3 11.9 %collective-permute-start.3 = (bf16[192,768]{1,0:T(8,128)(2,1)S(1)}, bf16[192,768]{1,0:T(8,128)(2,1)S(1)}, u32[]{:S(2)}, u32[]{:S(2)}) collective-permute-start(bf16[192,768]{1,0:T(8,128)(2,1)S(1)} %copy-done.43), channel_id=1, source_target_pairs={{0,1},{1,0},{2,3},{3,2},{4,5},{5,4},{6,7},{7,6},{8,9},{9,8},{10,11... | collective-permute-start | bytes 884744 | tf_op jit(solution)/shard_map/ppermute | solution.py:581
  22.5 14.5 %collective-permute-start.4 = (bf16[192,768]{1,0:T(8,128)(2,1)S(1)}, bf16[192,768]{1,0:T(8,128)(2,1)S(1)}, u32[]{:S(2)}, u32[]{:S(2)}) collective-permute-start(bf16[192,768]{1,0:T(8,128)(2,1)S(1)} %copy-done.41), channel_id=1, source_target_pairs={{0,1},{1,0},{2,3},{3,2},{4,5},{5,4},{6,7},{7,6},{8,9},{9,8},{10,11... | collective-permute-start | bytes 884744 | tf_op jit(solution)/shard_map/ppermute | solution.py:581
  33.2 32.0 %copy-start.22 = (bf16[1024,256]{1,0:T(8,128)(2,1)}, bf16[1024,256]{1,0:T(8,128)(2,1)S(1)}, u32[]{:S(2)}) copy-start(bf16[1024,256]{1,0:T(8,128)(2,1)S(1)} %get-tuple-element.210.refs_2_.refs_3_) | copy-start | bytes 1572868
  37.1 2.8 collective-permute-start.7
  37.1 21.4 %collective-permute-start.6 = (bf16[192,768]{1,0:T(8,128)(2,1)S(1)}, bf16[192,768]{1,0:T(8,128)(2,1)S(1)}, u32[]{:S(2)}, u32[]{:S(2)}) collective-permute-start(bf16[192,768]{1,0:T(8,128)(2,1)S(1)} %get-tuple-element.195), channel_id=1, source_target_pairs={{0,1},{1,0},{2,3},{3,2},{4,5},{5,4},{6,7},{7,6},{8,9},{9,8},{10,11... | collective-permute-start | bytes 884744 | tf_op jit(solution)/shard_map/ppermute | solution.py:581
  38.2 1.6 collective-permute-start.8
  49.1 16.1 %copy-start.24 = (bf16[1024,256]{1,0:T(8,128)(2,1)}, bf16[1024,256]{1,0:T(8,128)(2,1)S(1)}, u32[]{:S(2)}) copy-start(bf16[1024,256]{1,0:T(8,128)(2,1)S(1)} %get-tuple-element.211.refs_3_) | copy-start | bytes 1572868
  58.5 6.7 %collective-permute-start.9 = (bf16[1,192,768]{2,1,0:T(8,128)(2,1)S(1)}, bf16[1,192,768]{2,1,0:T(8,128)(2,1)S(1)}, u32[]{:S(2)}, u32[]{:S(2)}) collective-permute-start(bf16[1,192,768]{2,1,0:T(8,128)(2,1)S(1)} %bitcast.57), channel_id=1, source_target_pairs={{0,2},{2,0},{4,6},{6,4},{8,10},{10,8},{12,14},{14,12},{16,18},{18,... | collective-permute-start | bytes 884744 | tf_op jit(solution)/shard_map/ppermute | solution.py:581
  58.9 33.0 %collective-permute-start.10 = (bf16[2,384,768]{2,1,0:T(8,128)(2,1)S(1)}, bf16[2,384,768]{2,1,0:T(8,128)(2,1)S(1)}, u32[]{:S(2)}, u32[]{:S(2)}) collective-permute-start(bf16[2,384,768]{2,1,0:T(8,128)(2,1)S(1)} %pad_maximum_fusion), channel_id=1, source_target_pairs={{0,1},{1,0},{2,3},{3,2},{4,5},{5,4},{6,7},{7,6},{8,9},{9,8},{10,11... | collective-permute-start | bytes 3538952 | tf_op jit(solution)/shard_map/ppermute | solution.py:581
  65.1 51.9 %collective-permute-start.13 = (bf16[2,384,768]{2,1,0:T(8,128)(2,1)S(1)}, bf16[2,384,768]{2,1,0:T(8,128)(2,1)S(1)}, u32[]{:S(2)}, u32[]{:S(2)}) collective-permute-start(bf16[2,384,768]{2,1,0:T(8,128)(2,1)S(1)} %pad_maximum_fusion.1), channel_id=1, source_target_pairs={{0,1},{1,0},{2,3},{3,2},{4,5},{5,4},{6,7},{7,6},{8,9},{9,8},{10,11... | collective-permute-start | bytes 3538952 | tf_op jit(solution)/shard_map/ppermute | solution.py:581
  91.9 9.7 %collective-permute-start.11 = (bf16[1,2,384,768]{3,2,1,0:T(8,128)(2,1)S(1)}, bf16[1,2,384,768]{3,2,1,0:T(8,128)(2,1)S(1)}, u32[]{:S(2)}, u32[]{:S(2)}) collective-permute-start(bf16[1,2,384,768]{3,2,1,0:T(8,128)(2,1)S(1)} %bitcast.67), channel_id=1, source_target_pairs={{0,2},{2,0},{4,6},{6,4},{8,10},{10,8},{12,14},{14,12},{16,18},{18,... | collective-permute-start | bytes 3538952 | tf_op jit(solution)/shard_map/ppermute | solution.py:581
  117.0 2.8 collective-permute-start.14
  117.0 4.5 %collective-permute-start.12 = (bf16[768,768]{1,0:T(8,128)(2,1)S(1)}, bf16[768,768]{1,0:T(8,128)(2,1)S(1)}, u32[]{:S(2)}, u32[]{:S(2)}) collective-permute-start(bf16[768,768]{1,0:T(8,128)(2,1)S(1)} %get-tuple-element.230), channel_id=1, source_target_pairs={{0,2},{2,0},{4,6},{6,4},{8,10},{10,8},{12,14},{14,12},{16,18},{18,... | collective-permute-start | bytes 3538952 | tf_op jit(solution)/shard_map/ppermute | solution.py:581
  121.8 13.9 %collective-permute-start.15 = (bf16[768,768]{1,0:T(8,128)(2,1)}, bf16[768,768]{1,0:T(8,128)(2,1)}, u32[]{:S(2)}, u32[]{:S(2)}) collective-permute-start(bf16[768,768]{1,0:T(8,128)(2,1)} %get-tuple-element.244), channel_id=1, source_target_pairs={{0,2},{2,0},{4,6},{6,4},{8,10},{10,8},{12,14},{14,12},{16,18},{18,... | collective-permute-start | bytes 3538952 | tf_op jit(solution)/shard_map/ppermute | solution.py:581
  122.0 13.7 %collective-permute-start.16 = (bf16[768,768]{1,0:T(8,128)(2,1)}, bf16[768,768]{1,0:T(8,128)(2,1)}, u32[]{:S(2)}, u32[]{:S(2)}) collective-permute-start(bf16[768,768]{1,0:T(8,128)(2,1)} %get-tuple-element.248), channel_id=1, source_target_pairs={{0,2},{2,0},{4,6},{6,4},{8,10},{10,8},{12,14},{14,12},{16,18},{18,... | collective-permute-start | bytes 3538952 | tf_op jit(solution)/shard_map/ppermute | solution.py:581
  133.8 15.3 %collective-permute-start.17 = (bf16[768,768]{1,0:T(8,128)(2,1)}, bf16[768,768]{1,0:T(8,128)(2,1)}, u32[]{:S(2)}, u32[]{:S(2)}) collective-permute-start(bf16[768,768]{1,0:T(8,128)(2,1)} %get-tuple-element.242), channel_id=1, source_target_pairs={{0,2},{2,0},{4,6},{6,4},{8,10},{10,8},{12,14},{14,12},{16,18},{18,... | collective-permute-start | bytes 3538952 | tf_op jit(solution)/shard_map/ppermute | solution.py:581
  134.0 30.2 %collective-permute-start.19 = (bf16[768,768]{1,0:T(8,128)(2,1)S(1)}, bf16[768,768]{1,0:T(8,128)(2,1)S(1)}, u32[]{:S(2)}, u32[]{:S(2)}) collective-permute-start(bf16[768,768]{1,0:T(8,128)(2,1)S(1)} %combine.25), channel_id=1, source_target_pairs={{0,1},{1,0},{2,3},{3,2},{4,5},{5,4},{6,7},{7,6},{8,9},{9,8},{10,11... | collective-permute-start | bytes 3538952 | tf_op jit(solution)/shard_map/ppermute | solution.py:581
  151.5 30.4 %collective-permute-start.18 = (bf16[384,768]{1,0:T(8,128)(2,1)S(1)}, bf16[384,768]{1,0:T(8,128)(2,1)S(1)}, u32[]{:S(2)}, u32[]{:S(2)}) collective-permute-start(bf16[384,768]{1,0:T(8,128)(2,1)S(1)} %get-tuple-element.260), channel_id=1, source_target_pairs={{0,4},{2,6},{4,0},{6,2},{8,12},{10,14},{12,8},{14,10},{16,20},{18,... | collective-permute-start | bytes 1769480 | tf_op jit(solution)/shard_map/ppermute | solution.py:581
  152.4 29.2 %collective-permute-start.20 = (bf16[384,768]{1,0:T(8,128)(2,1)S(1)}, bf16[384,768]{1,0:T(8,128)(2,1)S(1)}, u32[]{:S(2)}, u32[]{:S(2)}) collective-permute-start(bf16[384,768]{1,0:T(8,128)(2,1)S(1)} %get-tuple-element.266), channel_id=1, source_target_pairs={{0,4},{2,6},{4,0},{6,2},{8,12},{10,14},{12,8},{14,10},{16,20},{18,... | collective-permute-start | bytes 1769480 | tf_op jit(solution)/shard_map/ppermute | solution.py:581
  164.1 21.6 %collective-permute-start.21 = (bf16[2,384,768]{2,1,0:T(8,128)(2,1)S(1)}, bf16[2,384,768]{2,1,0:T(8,128)(2,1)S(1)}, u32[]{:S(2)}, u32[]{:S(2)}) collective-permute-start(bf16[2,384,768]{2,1,0:T(8,128)(2,1)S(1)} %get-tuple-element.272), channel_id=1, source_target_pairs={{0,2},{2,0},{4,6},{6,4},{8,10},{10,8},{12,14},{14,12},{16,18},{18,... | collective-permute-start | bytes 3538952 | tf_op jit(solution)/shard_map/ppermute | solution.py:581
  166.1 37.7 %collective-permute-start.23 = (bf16[384,768]{1,0:T(8,128)(2,1)S(1)}, bf16[384,768]{1,0:T(8,128)(2,1)S(1)}, u32[]{:S(2)}, u32[]{:S(2)}) collective-permute-start(bf16[384,768]{1,0:T(8,128)(2,1)S(1)} %get-tuple-element.276), channel_id=1, source_target_pairs={{0,4},{2,6},{4,0},{6,2},{8,12},{10,14},{12,8},{14,10},{16,20},{18,... | collective-permute-start | bytes 1769480 | tf_op jit(solution)/shard_map/ppermute | solution.py:581
  181.9 18.1 %collective-permute-start.24 = (bf16[384,768]{1,0:T(8,128)(2,1)S(1)}, bf16[384,768]{1,0:T(8,128)(2,1)S(1)}, u32[]{:S(2)}, u32[]{:S(2)}) collective-permute-start(bf16[384,768]{1,0:T(8,128)(2,1)S(1)} %combine.28), channel_id=1, source_target_pairs={{0,1},{1,0},{2,3},{3,2},{4,5},{5,4},{6,7},{7,6},{8,9},{9,8},{10,11... | collective-permute-start | bytes 1769480 | tf_op jit(solution)/shard_map/ppermute | solution.py:581
  185.9 35.7 %collective-permute-start.25 = (bf16[384,768]{1,0:T(8,128)(2,1)S(1)}, bf16[384,768]{1,0:T(8,128)(2,1)S(1)}, u32[]{:S(2)}, u32[]{:S(2)}) collective-permute-start(bf16[384,768]{1,0:T(8,128)(2,1)S(1)} %combine.29), channel_id=1, source_target_pairs={{0,1},{1,0},{2,3},{3,2},{4,5},{5,4},{6,7},{7,6},{8,9},{9,8},{10,11... | collective-permute-start | bytes 1769480 | tf_op jit(solution)/shard_map/ppermute | solution.py:581
  187.3 16.8 %copy-start.34 = (bf16[768,768]{1,0:T(8,128)(2,1)S(1)}, bf16[768,768]{1,0:T(8,128)(2,1)}, u32[]{:S(2)}) copy-start(bf16[768,768]{1,0:T(8,128)(2,1)} %get-tuple-element.301.refs_8_) | copy-start | bytes 3538948
  187.3 16.8 %copy-start.35 = (bf16[768,768]{1,0:T(8,128)(2,1)S(1)}, bf16[768,768]{1,0:T(8,128)(2,1)}, u32[]{:S(2)}) copy-start(bf16[768,768]{1,0:T(8,128)(2,1)} %get-tuple-element.302.refs_9_) | copy-start | bytes 3538948
  187.3 16.8 %copy-start.46 = (bf16[1024,768]{1,0:T(8,128)(2,1)S(1)}, bf16[1024,768]{1,0:T(8,128)(2,1)}, u32[]{:S(2)}) copy-start(bf16[1024,768]{1,0:T(8,128)(2,1)} %get-tuple-element.297.refs_4_) | copy-start | bytes 4718596
  187.3 16.8 %copy-start.47 = (bf16[1024,768]{1,0:T(8,128)(2,1)S(1)}, bf16[1024,768]{1,0:T(8,128)(2,1)}, u32[]{:S(2)}) copy-start(bf16[1024,768]{1,0:T(8,128)(2,1)} %get-tuple-element.298.refs_5_) | copy-start | bytes 4718596
  200.2 20.2 %collective-permute-start.27 = (bf16[192,768]{1,0:T(8,128)(2,1)S(1)}, bf16[192,768]{1,0:T(8,128)(2,1)S(1)}, u32[]{:S(2)}, u32[]{:S(2)}) collective-permute-start(bf16[192,768]{1,0:T(8,128)(2,1)S(1)} %get-tuple-element.294), channel_id=1, source_target_pairs={{0,8},{2,10},{4,12},{6,14},{8,0},{10,2},{12,4},{14,6},{16,24},{18,... | collective-permute-start | bytes 884744 | tf_op jit(solution)/shard_map/ppermute | solution.py:581
  204.0 13.9 %collective-permute-start.26 = (bf16[192,768]{1,0:T(8,128)(2,1)S(1)}, bf16[192,768]{1,0:T(8,128)(2,1)S(1)}, u32[]{:S(2)}, u32[]{:S(2)}) collective-permute-start(bf16[192,768]{1,0:T(8,128)(2,1)S(1)} %get-tuple-element.291), channel_id=1, source_target_pairs={{0,8},{2,10},{4,12},{6,14},{8,0},{10,2},{12,4},{14,6},{16,24},{18,... | collective-permute-start | bytes 884744 | tf_op jit(solution)/shard_map/ppermute | solution.py:581
  204.1 19.4 %collective-permute-start.22 = (bf16[2,384,768]{2,1,0:T(8,128)(2,1)S(1)}, bf16[2,384,768]{2,1,0:T(8,128)(2,1)S(1)}, u32[]{:S(2)}, u32[]{:S(2)}) collective-permute-start(bf16[2,384,768]{2,1,0:T(8,128)(2,1)S(1)} %get-tuple-element.287), channel_id=1, source_target_pairs={{0,2},{2,0},{4,6},{6,4},{8,10},{10,8},{12,14},{14,12},{16,18},{18,... | collective-permute-start | bytes 3538952 | tf_op jit(solution)/shard_map/ppermute | solution.py:581
  205.6 19.2 %copy-start.50 = (bf16[1024,768]{1,0:T(8,128)(2,1)S(1)}, bf16[1024,768]{1,0:T(8,128)(2,1)}, u32[]{:S(2)}) copy-start(bf16[1024,768]{1,0:T(8,128)(2,1)} %get-tuple-element.314.refs_3_) | copy-start | bytes 4718596
  205.6 19.2 %copy-start.51 = (bf16[1024,768]{1,0:T(8,128)(2,1)S(1)}, bf16[1024,768]{1,0:T(8,128)(2,1)}, u32[]{:S(2)}) copy-start(bf16[1024,768]{1,0:T(8,128)(2,1)} %get-tuple-element.315.refs_4_) | copy-start | bytes 4718596
  205.6 19.2 %copy-start.52 = (bf16[1024,768]{1,0:T(8,128)(2,1)S(1)}, bf16[1024,768]{1,0:T(8,128)(2,1)}, u32[]{:S(2)}) copy-start(bf16[1024,768]{1,0:T(8,128)(2,1)} %get-tuple-element.316.refs_5_) | copy-start | bytes 4718596
  205.6 19.2 %copy-start.53 = (bf16[768,768]{1,0:T(8,128)(2,1)S(1)}, bf16[768,768]{1,0:T(8,128)(2,1)}, u32[]{:S(2)}) copy-start(bf16[768,768]{1,0:T(8,128)(2,1)} %get-tuple-element.317.refs_8_) | copy-start | bytes 3538948
  205.6 19.2 %copy-start.54 = (bf16[768,768]{1,0:T(8,128)(2,1)S(1)}, bf16[768,768]{1,0:T(8,128)(2,1)}, u32[]{:S(2)}) copy-start(bf16[768,768]{1,0:T(8,128)(2,1)} %get-tuple-element.318.refs_9_) | copy-start | bytes 3538948
  216.8 4.3 %collective-permute-start.28 = (f32[12,384]{1,0:T(8,128)S(1)}, f32[12,384]{1,0:T(8,128)S(1)}, u32[]{:S(2)}, u32[]{:S(2)}) collective-permute-start(f32[12,384]{1,0:T(8,128)S(1)} %get-tuple-element.352), channel_id=1, source_target_pairs={{0,1},{1,0},{2,3},{3,2},{4,5},{5,4},{6,7},{7,6},{8,9},{9,8},{10,11... | collective-permute-start | bytes 55304 | tf_op jit(solution)/shard_map/ppermute | solution.py:581
  218.0 23.5 %collective-permute-start.31 = (bf16[192,768]{1,0:T(8,128)(2,1)S(1)}, bf16[192,768]{1,0:T(8,128)(2,1)S(1)}, u32[]{:S(2)}, u32[]{:S(2)}) collective-permute-start(bf16[192,768]{1,0:T(8,128)(2,1)S(1)} %combine.34.refs_0_), channel_id=1, source_target_pairs={{0,16},{2,18},{4,20},{6,22},{8,24},{10,26},{12,28},{14,30},{16,0},... | collective-permute-start | bytes 884744 | tf_op jit(solution)/shard_map/ppermute | solution.py:581
  220.5 26.4 %collective-permute-start.33 = (bf16[192,768]{1,0:T(8,128)(2,1)S(1)}, bf16[192,768]{1,0:T(8,128)(2,1)S(1)}, u32[]{:S(2)}, u32[]{:S(2)}) collective-permute-start(bf16[192,768]{1,0:T(8,128)(2,1)S(1)} %combine.35.refs_0_), channel_id=1, source_target_pairs={{0,16},{2,18},{4,20},{6,22},{8,24},{10,26},{12,28},{14,30},{16,0},... | collective-permute-start | bytes 884744 | tf_op jit(solution)/shard_map/ppermute | solution.py:581
  221.1 16.0 %collective-permute-start.29 = (f32[12,384]{1,0:T(8,128)S(1)}, f32[12,384]{1,0:T(8,128)S(1)}, u32[]{:S(2)}, u32[]{:S(2)}) collective-permute-start(f32[12,384]{1,0:T(8,128)S(1)} %combine.36.refs_0_), channel_id=1, source_target_pairs={{0,4},{2,6},{4,0},{6,2},{8,12},{10,14},{12,8},{14,10},{16,20},{18,... | collective-permute-start | bytes 55304 | tf_op jit(solution)/shard_map/ppermute | solution.py:581
  221.8 19.8 %collective-permute-start.35 = (bf16[192,768]{1,0:T(8,128)(2,1)S(1)}, bf16[192,768]{1,0:T(8,128)(2,1)S(1)}, u32[]{:S(2)}, u32[]{:S(2)}) collective-permute-start(bf16[192,768]{1,0:T(8,128)(2,1)S(1)} %get-tuple-element.307), channel_id=1, source_target_pairs={{0,4},{2,6},{4,0},{6,2},{8,12},{10,14},{12,8},{14,10},{16,20},{18,... | collective-permute-start | bytes 884744 | tf_op jit(solution)/shard_map/ppermute | solution.py:581
  223.6 20.1 %collective-permute-start.34 = (bf16[384,768]{1,0:T(8,128)(2,1)S(1)}, bf16[384,768]{1,0:T(8,128)(2,1)S(1)}, u32[]{:S(2)}, u32[]{:S(2)}) collective-permute-start(bf16[384,768]{1,0:T(8,128)(2,1)S(1)} %combine.32), channel_id=1, source_target_pairs={{0,1},{1,0},{2,3},{3,2},{4,5},{5,4},{6,7},{7,6},{8,9},{9,8},{10,11... | collective-permute-start | bytes 1769480 | tf_op jit(solution)/shard_map/ppermute | solution.py:581
  241.5 11.6 %collective-permute-start.32 = (bf16[192,768]{1,0:T(8,128)(2,1)S(1)}, bf16[192,768]{1,0:T(8,128)(2,1)S(1)}, u32[]{:S(2)}, u32[]{:S(2)}) collective-permute-start(bf16[192,768]{1,0:T(8,128)(2,1)S(1)} %combine.38.part_ref), channel_id=1, source_target_pairs={{0,8},{2,10},{4,12},{6,14},{8,0},{10,2},{12,4},{14,6},{16,24},{18,... | collective-permute-start | bytes 884744 | tf_op jit(solution)/shard_map/ppermute | solution.py:581
  241.7 24.6 %collective-permute-start.37 = (bf16[192,768]{1,0:T(8,128)(2,1)S(1)}, bf16[192,768]{1,0:T(8,128)(2,1)S(1)}, u32[]{:S(2)}, u32[]{:S(2)}) collective-permute-start(bf16[192,768]{1,0:T(8,128)(2,1)S(1)} %combine.39.refs_0_), channel_id=1, source_target_pairs={{0,8},{2,10},{4,12},{6,14},{8,0},{10,2},{12,4},{14,6},{16,24},{18,... | collective-permute-start | bytes 884744 | tf_op jit(solution)/shard_map/ppermute | solution.py:581
  244.0 23.5 %collective-permute-start.41 = (bf16[192,768]{1,0:T(8,128)(2,1)S(1)}, bf16[192,768]{1,0:T(8,128)(2,1)S(1)}, u32[]{:S(2)}, u32[]{:S(2)}) collective-permute-start(bf16[192,768]{1,0:T(8,128)(2,1)S(1)} %get-tuple-element.324), channel_id=1, source_target_pairs={{0,4},{2,6},{4,0},{6,2},{8,12},{10,14},{12,8},{14,10},{16,20},{18,... | collective-permute-start | bytes 884744 | tf_op jit(solution)/shard_map/ppermute | solution.py:581
  246.9 20.7 %collective-permute-start.43 = (bf16[192,768]{1,0:T(8,128)(2,1)S(1)}, bf16[192,768]{1,0:T(8,128)(2,1)S(1)}, u32[]{:S(2)}, u32[]{:S(2)}) collective-permute-start(bf16[192,768]{1,0:T(8,128)(2,1)S(1)} %combine.41.part_ref), channel_id=1, source_target_pairs={{0,8},{2,10},{4,12},{6,14},{8,0},{10,2},{12,4},{14,6},{16,24},{18,... | collective-permute-start | bytes 884744 | tf_op jit(solution)/shard_map/ppermute | solution.py:581
  253.2 29.0 %collective-permute-start.40 = (bf16[384,768]{1,0:T(8,128)(2,1)S(1)}, bf16[384,768]{1,0:T(8,128)(2,1)S(1)}, u32[]{:S(2)}, u32[]{:S(2)}) collective-permute-start(bf16[384,768]{1,0:T(8,128)(2,1)S(1)} %join.6.part_ref), channel_id=1, source_target_pairs={{0,4},{2,6},{4,0},{6,2},{8,12},{10,14},{12,8},{14,10},{16,20},{18,... | collective-permute-start | bytes 1769480 | tf_op jit(solution)/shard_map/ppermute | solution.py:581
  254.1 12.1 %collective-permute-start.30 = (f32[12,384]{1,0:T(8,128)S(1)}, f32[12,384]{1,0:T(8,128)S(1)}, u32[]{:S(2)}, u32[]{:S(2)}) collective-permute-start(f32[12,384]{1,0:T(8,128)S(1)} %combine.37.refs_0_), channel_id=1, source_target_pairs={{0,8},{2,10},{4,12},{6,14},{8,0},{10,2},{12,4},{14,6},{16,24},{18,... | collective-permute-start | bytes 55304 | tf_op jit(solution)/shard_map/ppermute | solution.py:581
  266.3 1.2 collective-permute-start.36
  267.5 14.5 %collective-permute-start.42 = (bf16[192,768]{1,0:T(8,128)(2,1)S(1)}, bf16[192,768]{1,0:T(8,128)(2,1)S(1)}, u32[]{:S(2)}, u32[]{:S(2)}) collective-permute-start(bf16[192,768]{1,0:T(8,128)(2,1)S(1)} %combine.45.refs_0_), channel_id=1, source_target_pairs={{0,8},{2,10},{4,12},{6,14},{8,0},{10,2},{12,4},{14,6},{16,24},{18,... | collective-permute-start | bytes 884744 | tf_op jit(solution)/shard_map/ppermute | solution.py:581
  267.7 31.9 %collective-permute-start.45 = (bf16[384,768]{1,0:T(8,128)(2,1)S(1)}, bf16[384,768]{1,0:T(8,128)(2,1)S(1)}, u32[]{:S(2)}, u32[]{:S(2)}) collective-permute-start(bf16[384,768]{1,0:T(8,128)(2,1)S(1)} %join.7.part_ref), channel_id=1, source_target_pairs={{0,4},{2,6},{4,0},{6,2},{8,12},{10,14},{12,8},{14,10},{16,20},{18,... | collective-permute-start | bytes 1769480 | tf_op jit(solution)/shard_map/ppermute | solution.py:581
  268.6 24.4 %collective-permute-start.39 = (bf16[192,768]{1,0:T(8,128)(2,1)S(1)}, bf16[192,768]{1,0:T(8,128)(2,1)S(1)}, u32[]{:S(2)}, u32[]{:S(2)}) collective-permute-start(bf16[192,768]{1,0:T(8,128)(2,1)S(1)} %combine.43.refs_0_), channel_id=1, source_target_pairs={{0,16},{2,18},{4,20},{6,22},{8,24},{10,26},{12,28},{14,30},{16,0},... | collective-permute-start | bytes 884744 | tf_op jit(solution)/shard_map/ppermute | solution.py:581
  282.1 17.4 %collective-permute-start.46 = (bf16[192,768]{1,0:T(8,128)(2,1)S(1)}, bf16[192,768]{1,0:T(8,128)(2,1)S(1)}, u32[]{:S(2)}, u32[]{:S(2)}) collective-permute-start(bf16[192,768]{1,0:T(8,128)(2,1)S(1)} %combine.46.refs_0_), channel_id=1, source_target_pairs={{0,16},{2,18},{4,20},{6,22},{8,24},{10,26},{12,28},{14,30},{16,0},... | collective-permute-start | bytes 884744 | tf_op jit(solution)/shard_map/ppermute | solution.py:581
  293.1 6.8 %collective-permute-start.44 = (bf16[192,768]{1,0:T(8,128)(2,1)S(1)}, bf16[192,768]{1,0:T(8,128)(2,1)S(1)}, u32[]{:S(2)}, u32[]{:S(2)}) collective-permute-start(bf16[192,768]{1,0:T(8,128)(2,1)S(1)} %combine.47.part_ref), channel_id=1, source_target_pairs={{0,4},{2,6},{4,0},{6,2},{8,12},{10,14},{12,8},{14,10},{16,20},{18,... | collective-permute-start | bytes 884744 | tf_op jit(solution)/shard_map/ppermute | solution.py:581
  294.5 5.0 %collective-permute-start.38 = (f32[12,384]{1,0:T(8,128)S(1)}, f32[12,384]{1,0:T(8,128)S(1)}, u32[]{:S(2)}, u32[]{:S(2)}) collective-permute-start(f32[12,384]{1,0:T(8,128)S(1)} %combine.44.refs_0_), channel_id=1, source_target_pairs={{0,16},{2,18},{4,20},{6,22},{8,24},{10,26},{12,28},{14,30},{16,0},... | collective-permute-start | bytes 55304 | tf_op jit(solution)/shard_map/ppermute | solution.py:581
  299.9 10.7 %collective-permute-start.47 = (bf16[384,768]{1,0:T(8,128)(2,1)S(1)}, bf16[384,768]{1,0:T(8,128)(2,1)}, u32[]{:S(2)}, u32[]{:S(2)}) collective-permute-start(bf16[384,768]{1,0:T(8,128)(2,1)S(1)} %join.10), channel_id=1, source_target_pairs={{0,2},{2,0},{4,6},{6,4},{8,10},{10,8},{12,14},{14,12},{16,18},{18,... | collective-permute-start | bytes 1769480 | tf_op jit(solution)/shard_map/ppermute | solution.py:581
  300.0 9.5 %collective-permute-start.48 = (bf16[192,768]{1,0:T(8,128)(2,1)S(1)}, bf16[192,768]{1,0:T(8,128)(2,1)}, u32[]{:S(2)}, u32[]{:S(2)}) collective-permute-start(bf16[192,768]{1,0:T(8,128)(2,1)S(1)} %combine.49.part_ref), channel_id=1, source_target_pairs={{0,4},{2,6},{4,0},{6,2},{8,12},{10,14},{12,8},{14,10},{16,20},{18,... | collective-permute-start | bytes 884744 | tf_op jit(solution)/shard_map/ppermute | solution.py:581
  301.6 13.7 %collective-permute-start.50 = (bf16[768,768]{1,0:T(8,128)(2,1)S(1)}, bf16[768,768]{1,0:T(8,128)(2,1)}, u32[]{:S(2)}, u32[]{:S(2)}) collective-permute-start(bf16[768,768]{1,0:T(8,128)(2,1)S(1)} %join.8), channel_id=1, source_target_pairs={{0,2},{2,0},{4,6},{6,4},{8,10},{10,8},{12,14},{14,12},{16,18},{18,... | collective-permute-start | bytes 3538952 | tf_op jit(solution)/shard_map/ppermute | solution.py:581
  303.0 13.8 %collective-permute-start.51 = (bf16[768,768]{1,0:T(8,128)(2,1)S(1)}, bf16[768,768]{1,0:T(8,128)(2,1)S(1)}, u32[]{:S(2)}, u32[]{:S(2)}) collective-permute-start(bf16[768,768]{1,0:T(8,128)(2,1)S(1)} %join.9), channel_id=1, source_target_pairs={{0,2},{2,0},{4,6},{6,4},{8,10},{10,8},{12,14},{14,12},{16,18},{18,... | collective-permute-start | bytes 3538952 | tf_op jit(solution)/shard_map/ppermute | solution.py:581
  310.5 2.4 collective-permute-start.49
  (48 other events, 192.5 us)
where the time goes:
time: 329 us; the launch traced here: 323 us
  Pallas kernels  139 us (42%)
  waiting for transfers between devices  90.4 us (27%)
  starting transfers between devices  52.9 us (16%)
  local copies, waits for them, and re-layouts  26.6 us (8%)
  other arithmetic  11.9 us (4%)
    ppermute x52, waiting for transfers between devices, swap(): return lax.ppermute(value, axis, [(i, i ^ bit) for i in range(size)])  90.4 us
    ppermute x52, starting transfers between devices, swap(): return lax.ppermute(value, axis, [(i, i ^ bit) for i in range(size)])  52.9 us
    pallas_call x4, Pallas kernels, ffn(): call(functools.partial(ffn_kernel, own, apart, fresh, offset), 'ffn', out...  32.8 us
    pallas_call x3, Pallas kernels, attn_bwd(): call(functools.partial(attn_bwd_kernel, dh, bool(extra)), 'attn_bwd', (ar...  32.2 us
    pallas_call x3, Pallas kernels, attn_fwd(): call(functools.partial(attn_fwd_kernel, dh), 'attn_fwd', (array((d, 3 * w...  28.4 us
    unnamed x135, local copies, waits for them, and re-layouts  24.9 us
    pallas_call x1, Pallas kernels, result(): call(functools.partial(result_kernel, n, offsets), 'result', array((rows,...  11.9 us
    pallas_call x1, Pallas kernels, leave(): call(functools.partial(leave_kernel, shards, len(ups)), 'leave', (array((...  11.2 us
  transfers between devices with their start and end apart: 52, of which 18 were waited for; matrix products, arithmetic and copies ran while one was open for 3% of the time, Pallas kernels for 42%

commit v1 on v0

--- a/solution.py
+++ b/solution.py
@@ -901,14 +901,14 @@
     for i in tail:
         add_far(i)
     join_next(0, z, x)
-    small = add_step([small], small_got)
-    small_got = ring.swap(small, 1)
+    two = add_step([keep], two_got)
+    two_got = ring.swap(two, z)
     one = add_step([one], one_got)
     one_got = ring.swap(one, far_bit)
     small = add_step([small], small_got)
+    small_got = ring.swap(small, 1)
+    small = add_step([small], small_got)
     small_got = ring.swap(small, far_bit)
-    two = add_step([keep], two_got)
-    two_got = ring.swap(two, z)
     for i in tail:
         join_next(i, z, x)
     two = add_step([two], two_got)

time: 329 us -> 328 us (level)
  transfers between devices with their start and end apart: 52 -> 52, of which waited for: 18 -> 20; matrix products, arithmetic and copies ran while one was open for 3% -> 3% of each run, Pallas kernels for 42% -> 43%
where the time goes in v1:
time: 328 us; the launch traced here: 322 us
  Pallas kernels  139 us (42%)
  waiting for transfers between devices  92.7 us (28%)
  starting transfers between devices  49.7 us (15%)
  local copies, waits for them, and re-layouts  26.7 us (8%)
  other arithmetic  11.9 us (4%)
    ppermute x52, waiting for transfers between devices, swap(): return lax.ppermute(value, axis, [(i, i ^ bit) for i in range(size)])  92.7 us
    ppermute x52, starting transfers between devices, swap(): return lax.ppermute(value, axis, [(i, i ^ bit) for i in range(size)])  49.7 us
    pallas_call x4, Pallas kernels, ffn(): call(functools.partial(ffn_kernel, own, apart, fresh, offset), 'ffn', out...  32.8 us
    pallas_call x3, Pallas kernels, attn_bwd(): call(functools.partial(attn_bwd_kernel, dh, bool(extra)), 'attn_bwd', (ar...  32.2 us
    pallas_call x3, Pallas kernels, attn_fwd(): call(functools.partial(attn_fwd_kernel, dh), 'attn_fwd', (array((d, 3 * w...  28.4 us
    unnamed x135, local copies, waits for them, and re-layouts  25 us
    pallas_call x1, Pallas kernels, result(): call(functools.partial(result_kernel, n, offsets), 'result', array((rows,...  11.9 us
    pallas_call x1, Pallas kernels, leave(): call(functools.partial(leave_kernel, shards, len(ups)), 'leave', (array((...  11.2 us
  transfers between devices with their start and end apart: 52, of which 20 were waited for; matrix products, arithmetic and copies ran while one was open for 3% of the time, Pallas kernels for 43%

profile of v1, /device:TPU:0, one launch (start us, length us, event | category | flops | bytes accessed | tf_op | source)
XLA Modules:
  0.0 321.9 jit_solution(10924107453525579471)
XLA Ops:
  0.8 1.6 copy-done.8
  2.4 1.4 pack.1
  6.8 3.0 collective-permute-start
  10.0 2.1 collective-permute-start.1
  12.7 1.7 copy-done.3
  14.3 1.7 copy-done.5
  17.9 3.3 %enter.1 = (bf16[1024,768]{1,0:T(8,128)(2,1)S(1)}, bf16[768,1024]{1,0:T(8,128)(2,1)}, f32[1,768]{1,0:T(1,128)S(1)}, f32[8,768]{1,0:T(8,128)S(1)}, f32[1,768]{1,0...) custom-call(s32[2]{0:T(128)S(1)} %pad_add_fusion.1.pos_ref.refs_0_, bf16[1024,768]{1,0:T(8,128)(2,1)S(1)} %copy-done, ...), custom_call_target="tpu_custom_call" | custom-call | flops 62914560 | bytes 25165824 | tf_op jit(solution)/shard_map/enter/pallas_call | solution.py:134
  21.3 1.2 collective-permute-start.3
  23.5 9.8 %attn_fwd.3 = (bf16[768,768]{1,0:T(8,128)(2,1)}, bf16[1024,768]{1,0:T(8,128)(2,1)}, bf16[1024,256]{1,0:T(8,128)(2,1)S(1)}, bf16[256,1024]{1,0:T(8,128)(2,1)}, f32[1,4096]{1,0:T(1,128)S(1)}) custom-call(s32[2]{0:T(128)S(1)} %pad_add_fusion.1.pos_ref.refs_0_, s32[2,4]{1,0:T(2,128)S(1)} %pad_add_fusion.refs_1_, ...), custom_call_target="tpu_custom_call" | custom-call | flops 335544320 | bytes 471859 | tf_op jit(solution)/shard_map/attn_fwd/pallas_call | solution.py:273
  33.2 3.8 %collective-permute-done.4 = bf16[192,768]{1,0:T(8,128)(2,1)S(1)} collective-permute-done((bf16[192,768]{1,0:T(8,128)(2,1)S(1)}, bf16[192,768]{1,0:T(8,128)(2,1)S(1)}, u32[]{:S(2)}, u32[]{:S(2)}) %collective-permute-start.4) | collective-permute-done | bytes 294944 | tf_op jit(solution)/shard_map/ppermute | solution.py:581
  37.1 1.2 collective-permute-start.6
  38.6 1.2 collective-permute-done.8.refs_5_
  39.8 9.3 %attn_fwd.4 = (bf16[768,768]{1,0:T(8,128)(2,1)}, bf16[1024,768]{1,0:T(8,128)(2,1)}, bf16[1024,256]{1,0:T(8,128)(2,1)S(1)}, bf16[256,1024]{1,0:T(8,128)(2,1)}, f32[1,4096]{1,0:T(1,128)S(1)}) custom-call(s32[2]{0:T(128)S(1)} %pad_add_fusion.1.pos_ref.refs_0_, s32[2,4]{1,0:T(2,128)S(1)} %pad_add_fusion.refs_1_, ...), custom_call_target="tpu_custom_call" | custom-call | flops 335544320 | bytes 471859 | tf_op jit(solution)/shard_map/attn_fwd/pallas_call | solution.py:273
  49.1 9.3 %attn_fwd.5 = (bf16[768,768]{1,0:T(8,128)(2,1)}, bf16[1024,768]{1,0:T(8,128)(2,1)}, bf16[1024,256]{1,0:T(8,128)(2,1)S(1)}, bf16[256,1024]{1,0:T(8,128)(2,1)}, f32[1,4096]{1,0:T(1,128)S(1)}) custom-call(s32[2]{0:T(128)S(1)} %pad_add_fusion.1.pos_ref.refs_0_, s32[2,4]{1,0:T(2,128)S(1)} %pad_add_fusion.refs_1_, ...), custom_call_target="tpu_custom_call" | custom-call | flops 335544320 | bytes 471859 | tf_op jit(solution)/shard_map/attn_fwd/pallas_call | solution.py:273
  58.5 4.4 %collective-permute-start.9 = (bf16[1,192,768]{2,1,0:T(8,128)(2,1)S(1)}, bf16[1,192,768]{2,1,0:T(8,128)(2,1)S(1)}, u32[]{:S(2)}, u32[]{:S(2)}) collective-permute-start(bf16[1,192,768]{2,1,0:T(8,128)(2,1)S(1)} %bitcast.57), channel_id=1, source_target_pairs={{0,2},{2,0},{4,6},{6,4},{8,10},{10,8},{12,14},{14,12},{16,18},{18,... | collective-permute-start | bytes 884744 | tf_op jit(solution)/shard_map/ppermute | solution.py:581
  63.0 2.1 collective-permute-start.10
  65.2 4.0 %middle.1 = (bf16[768,768]{1,0:T(8,128)(2,1)}, f32[1024,768]{1,0:T(8,128)}, bf16[1024,768]{1,0:T(8,128)(2,1)S(1)}, bf16[768,1024]{1,0:T(8,128)(2,1)S(1)}) custom-call(s32[2]{0:T(128)S(1)} %pad_add_fusion.1.pos_ref.refs_0_, bf16[1024,768]{1,0:T(8,128)(2,1)S(1)} %copy-done, bf16[1024,256]{1,0:T(8,128)(2,1)S(1)} %get-tuple-element.210.refs_2_.refs_3_, ...), custom_call_target="tpu_custom_call" | custom-call | flops 120795952 | bytes 943718 | tf_op jit(solution)/shard_map/middle/pallas_call | solution.py:389
  69.2 8.2 %ffn.4 = (bf16[1024,768]{1,0:T(8,128)(2,1)}, bf16[768,768]{1,0:T(8,128)(2,1)S(1)}, bf16[768,768]{1,0:T(8,128)(2,1)}, f32[1,768]{1,0:T(1,128)S(1)}, f32[1024,768]{1,0:T(8,128)S(1)}) custom-call(s32[2]{0:T(128)S(1)} %pad_add_fusion.1.pos_ref.refs_0_, bf16[1024,768]{1,0:T(8,128)(2,1)S(1)} %get-tuple-element.239.refs_1_, ...), custom_call_target="tpu_custom_call" | custom-call | flops 24159191040 | bytes 62914560 | tf_op jit(solution)/shard_map/ffn/pallas_call | solution.py:456
  78.4 13.5 %collective-permute-done.10 = bf16[2,384,768]{2,1,0:T(8,128)(2,1)S(1)} collective-permute-done((bf16[2,384,768]{2,1,0:T(8,128)(2,1)S(1)}, bf16[2,384,768]{2,1,0:T(8,128)(2,1)S(1)}, u32[]{:S(2)}, u32[]{:S(2)}) %collective-permute-start.10) | collective-permute-done | bytes 1179680 | tf_op jit(solution)/shard_map/ppermute | solution.py:581
  91.9 8.7 %ffn.5 = (bf16[1024,768]{1,0:T(8,128)(2,1)}, bf16[768,768]{1,0:T(8,128)(2,1)S(1)}, bf16[768,768]{1,0:T(8,128)(2,1)}, f32[1,768]{1,0:T(1,128)S(1)}, f32[1024,768]{1,0:T(8,128)S(1)}) custom-call(s32[2]{0:T(128)S(1)} %pad_add_fusion.1.pos_ref.refs_0_, bf16[1024,768]{1,0:T(8,128)(2,1)S(1)} %get-tuple-element.239.refs_1_, ...), custom_call_target="tpu_custom_call" | custom-call | flops 24159191040 | bytes 62914560 | tf_op jit(solution)/shard_map/ffn/pallas_call | solution.py:456
  101.6 7.3 %ffn.6 = (bf16[1024,768]{1,0:T(8,128)(2,1)}, bf16[768,768]{1,0:T(8,128)(2,1)S(1)}, bf16[768,768]{1,0:T(8,128)(2,1)S(1)}, f32[1,768]{1,0:T(1,128)S(1)}, f32[1024,...) custom-call(s32[2]{0:T(128)S(1)} %pad_add_fusion.1.pos_ref.refs_0_, bf16[1024,768]{1,0:T(8,128)(2,1)S(1)} %get-tuple-element.239.refs_1_, ...), custom_call_target="tpu_custom_call" | custom-call | flops 24159191040 | bytes 62914560 | tf_op jit(solution)/shard_map/ffn/pallas_call | solution.py:456
  108.9 8.1 %collective-permute-done.13 = bf16[2,384,768]{2,1,0:T(8,128)(2,1)S(1)} collective-permute-done((bf16[2,384,768]{2,1,0:T(8,128)(2,1)S(1)}, bf16[2,384,768]{2,1,0:T(8,128)(2,1)S(1)}, u32[]{:S(2)}, u32[]{:S(2)}) %collective-permute-start.13) | collective-permute-done | bytes 1179680 | tf_op jit(solution)/shard_map/ppermute | solution.py:581
  117.5 2.3 collective-permute-done.14
  119.8 1.7 collective-permute-done.12.refs_1_
  122.4 8.7 %ffn.7 = (bf16[1024,768]{1,0:T(8,128)(2,1)}, bf16[768,768]{1,0:T(8,128)(2,1)S(1)}, bf16[768,768]{1,0:T(8,128)(2,1)}, f32[1,768]{1,0:T(1,128)S(1)}, f32[1024,768]{1,0:T(8,128)S(1)}, /*index=5*/bf16[768,768]{1,0:T(8,128)(2,1)}) custom-call(s32[2]{0:T(128)S(1)} %pad_add_fusion.1.pos_ref.refs_0_, bf16[1024,768]{1,0:T(8,128)(2,1)S(1)} %get-tuple-element.239.refs_1_, ...), custom_call_target="tpu_custom_call" | custom-call | flops 24159191040 | bytes 62914560 | tf_op jit(solution)/shard_map/ffn/pallas_call | solution.py:456
  132.2 1.7 copy-done.44
  134.0 1.8 collective-permute-start.19
  135.8 1.9 copy-done.27
  137.6 1.3 copy-done.36
  142.0 1.9 copy-done.45
  143.9 5.2 %turn.1 = (f32[1024,768]{1,0:T(8,128)S(1)}, bf16[1024,256]{1,0:T(8,128)(2,1)S(1)}, bf16[1024,256]{1,0:T(8,128)(2,1)S(1)}, bf16[1024,256]{1,0:T(8,128)(2,1)S(1)},...) custom-call(s32[2]{0:T(128)S(1)} %pad_add_fusion.1.pos_ref.refs_0_, ...), custom_call_target="tpu_custom_call" | custom-call | flops 9663676416 | bytes 62914560 | tf_op jit(solution)/shard_map/turn/pallas_call | solution.py:494
  149.2 2.3 combine.26
  151.7 1.9 collective-permute-start.20
  153.6 10.5 %attn_bwd.3 = (bf16[1024,768]{1,0:T(8,128)(2,1)}, bf16[2,384,768]{2,1,0:T(8,128)(2,1)S(1)}, bf16[2,384,768]{2,1,0:T(8,128)(2,1)S(1)}, f32[1,768]{1,0:T(1,128)S(1)}) custom-call(s32[2]{0:T(128)S(1)} %pad_add_fusion.1.pos_ref.refs_0_, s32[2,4]{1,0:T(2,128)S(1)} %pad_add_fusion.refs_1_, bf16[1024,768]{1,0:T(8,128)(2,1)S(1)} %copy-done.31, ...), custom_call_target="tpu_custom_call" | custom-call | flops 26306674688 | bytes 23068672 | tf_op jit(solution)/shard_map/attn_bwd/pallas_call | solution.py:360
  164.1 2.3 collective-permute-start.21
  166.4 1.8 combine.27
  168.9 11.2 %attn_bwd.4 = (bf16[1024,768]{1,0:T(8,128)(2,1)}, bf16[2,192,768]{2,1,0:T(8,128)(2,1)S(1)}, bf16[2,192,768]{2,1,0:T(8,128)(2,1)S(1)}, f32[1,768]{1,0:T(1,128)S(1)}) custom-call(s32[2]{0:T(128)S(1)} %pad_add_fusion.1.pos_ref.refs_0_, s32[2,4]{1,0:T(2,128)S(1)} %pad_add_fusion.refs_1_, bf16[1024,768]{1,0:T(8,128)(2,1)S(1)} %copy-done.32, ...), custom_call_target="tpu_custom_call" | custom-call | flops 26306674688 | bytes 23068672 | tf_op jit(solution)/shard_map/attn_bwd/pallas_call | solution.py:360
  180.5 4.5 %collective-permute-start.24 = (bf16[384,768]{1,0:T(8,128)(2,1)S(1)}, bf16[384,768]{1,0:T(8,128)(2,1)S(1)}, u32[]{:S(2)}, u32[]{:S(2)}) collective-permute-start(bf16[384,768]{1,0:T(8,128)(2,1)S(1)} %combine.28), channel_id=1, source_target_pairs={{0,1},{1,0},{2,3},{3,2},{4,5},{5,4},{6,7},{7,6},{8,9},{9,8},{10,11... | collective-permute-start | bytes 1769480 | tf_op jit(solution)/shard_map/ppermute | solution.py:581
  186.6 10.5 %attn_bwd.5 = (bf16[1024,768]{1,0:T(8,128)(2,1)}, bf16[2,384,768]{2,1,0:T(8,128)(2,1)S(1)}, bf16[2,384,768]{2,1,0:T(8,128)(2,1)S(1)}, f32[1,768]{1,0:T(1,128)S(1)}) custom-call(s32[2]{0:T(128)S(1)} %pad_add_fusion.1.pos_ref.refs_0_, s32[2,4]{1,0:T(2,128)S(1)} %pad_add_fusion.refs_1_, bf16[1024,768]{1,0:T(8,128)(2,1)S(1)} %copy-done.30, ...), custom_call_target="tpu_custom_call" | custom-call | flops 26306674688 | bytes 23068672 | tf_op jit(solution)/shard_map/attn_bwd/pallas_call | solution.py:360
  197.1 2.0 collective-permute-done.24.refs_2_
  199.3 3.5 %collective-permute-start.27 = (bf16[192,768]{1,0:T(8,128)(2,1)S(1)}, bf16[192,768]{1,0:T(8,128)(2,1)S(1)}, u32[]{:S(2)}, u32[]{:S(2)}) collective-permute-start(bf16[192,768]{1,0:T(8,128)(2,1)S(1)} %get-tuple-element.294), channel_id=1, source_target_pairs={{0,8},{2,10},{4,12},{6,14},{8,0},{10,2},{12,4},{14,6},{16,24},{18,... | collective-permute-start | bytes 884744 | tf_op jit(solution)/shard_map/ppermute | solution.py:581
  203.2 1.4 copy-done.48
  204.6 11.2 %leave.1 = (f32[1024,768]{1,0:T(8,128)}, f32[2,12,384]{2,1,0:T(8,128)S(1)}) custom-call(s32[2]{0:T(128)S(1)} %pad_add_fusion.1.pos_ref.refs_0_, bf16[1024,768]{1,0:T(8,128)(2,1)S(1)} %copy-done.1, f32[1024,768]{1,0:T(8,128)S(1)} %get-tuple-element.296.refs_2_, f32[8,768]{1,0:T(8,128)S(1)} %get-tuple-element.213.refs_8_.whole_ref.refs_3_.refs_1_, ...), custom_call_target="tpu_custom_call" | custom-call | flops 14495514624 | bytes 50331648 | tf_op jit(solution)/shard_map/leave/pallas_call | solution.py:546
  215.8 2.2 collective-permute-start.28
  218.1 2.5 collective-permute-start.32
  221.6 2.0 collective-permute-start.31
  225.3 11.9 %result.1 = bf16[1024,768]{1,0:T(8,128)(2,1)} custom-call(f32[1024,768]{1,0:T(8,128)S(1)} %copy-done.28, f32[8,768]{1,0:T(8,128)S(1)} %get-tuple-element.213.refs_8_.whole_ref.refs_3_.refs_1_, bf16[1024,768]{1,0:T(8,128)(2,1)S(1)} %copy-done.49, bf16[1024,768]{1,0:T(8,128)(2,1)S(1)} %copy-done.50, bf16[1024,768]{1,0:T(8,128)(2,1)S(1)} %copy-done.51, ...), custom_call_target="tpu_custom_call" | custom-call | flops 19327352832 | bytes 44040192 | tf_op jit(solution)/shard_map/result/pallas_call | solution.py:574
  237.3 4.3 %collective-permute-done.32.refs_1_ = bf16[192,768]{1,0:T(8,128)(2,1)S(1)} collective-permute-done((bf16[192,768]{1,0:T(8,128)(2,1)S(1)}, bf16[192,768]{1,0:T(8,128)(2,1)S(1)}, u32[]{:S(2)}, u32[]{:S(2)}) %collective-permute-start.32) | collective-permute-done | bytes 294944 | tf_op jit(solution)/shard_map/ppermute | solution.py:581
  242.4 1.9 collective-permute-start.33
  244.2 3.1 collective-permute-done.37.refs_1_
  247.4 6.2 %collective-permute-done.36.other_ref = bf16[192,768]{1,0:T(8,128)(2,1)S(1)} collective-permute-done((bf16[192,768]{1,0:T(8,128)(2,1)S(1)}, bf16[192,768]{1,0:T(8,128)(2,1)S(1)}, u32[]{:S(2)}, u32[]{:S(2)}) %collective-permute-start.36) | collective-permute-done | bytes 294944 | tf_op jit(solution)/shard_map/ppermute | solution.py:581
  253.9 6.0 %collective-permute-done.33.refs_1_ = bf16[192,768]{1,0:T(8,128)(2,1)S(1)} collective-permute-done((bf16[192,768]{1,0:T(8,128)(2,1)S(1)}, bf16[192,768]{1,0:T(8,128)(2,1)S(1)}, u32[]{:S(2)}, u32[]{:S(2)}) %collective-permute-start.33) | collective-permute-done | bytes 294944 | tf_op jit(solution)/shard_map/ppermute | solution.py:581
  260.0 6.7 %collective-permute-done.30.refs_1_ = f32[12,384]{1,0:T(8,128)S(1)} collective-permute-done((f32[12,384]{1,0:T(8,128)S(1)}, f32[12,384]{1,0:T(8,128)S(1)}, u32[]{:S(2)}, u32[]{:S(2)}) %collective-permute-start.30) | collective-permute-done | bytes 18464 | tf_op jit(solution)/shard_map/ppermute | solution.py:581
  268.2 2.8 collective-permute-start.40
  270.9 9.7 %collective-permute-done.42.refs_1_ = bf16[192,768]{1,0:T(8,128)(2,1)S(1)} collective-permute-done((bf16[192,768]{1,0:T(8,128)(2,1)S(1)}, bf16[192,768]{1,0:T(8,128)(2,1)S(1)}, u32[]{:S(2)}, u32[]{:S(2)}) %collective-permute-start.42) | collective-permute-done | bytes 294944 | tf_op jit(solution)/shard_map/ppermute | solution.py:581
  280.8 10.8 %collective-permute-done.40.refs_1_ = bf16[192,768]{1,0:T(8,128)(2,1)S(1)} collective-permute-done((bf16[192,768]{1,0:T(8,128)(2,1)S(1)}, bf16[192,768]{1,0:T(8,128)(2,1)S(1)}, u32[]{:S(2)}, u32[]{:S(2)}) %collective-permute-start.40) | collective-permute-done | bytes 294944 | tf_op jit(solution)/shard_map/ppermute | solution.py:581
  291.7 1.9 collective-permute-start.44
  293.6 4.7 %collective-permute-done.39.refs_1_ = f32[12,384]{1,0:T(8,128)S(1)} collective-permute-done((f32[12,384]{1,0:T(8,128)S(1)}, f32[12,384]{1,0:T(8,128)S(1)}, u32[]{:S(2)}, u32[]{:S(2)}) %collective-permute-start.39) | collective-permute-done | bytes 18464 | tf_op jit(solution)/shard_map/ppermute | solution.py:581
  299.1 1.6 collective-permute-start.48
  302.4 6.3 %collective-permute-done.48.other_ref = bf16[192,768]{1,0:T(8,128)(2,1)} collective-permute-done((bf16[192,768]{1,0:T(8,128)(2,1)S(1)}, bf16[192,768]{1,0:T(8,128)(2,1)}, u32[]{:S(2)}, u32[]{:S(2)}) %collective-permute-start.48) | collective-permute-done | bytes 294944 | tf_op jit(solution)/shard_map/ppermute | solution.py:581
  312.4 2.0 maximum_convert_fusion.2
  314.5 1.4 broadcast_select_fusion.1
  316.1 2.5 maximum_convert_fusion.1
  318.6 2.8 maximum_convert_fusion
  (252 shorter events, 30.6 us)
Async XLA Ops:
  6.8 14.4 %collective-permute-start = (bf16[192,768]{1,0:T(8,128)(2,1)}, bf16[192,768]{1,0:T(8,128)(2,1)}, u32[]{:S(2)}, u32[]{:S(2)}) collective-permute-start(bf16[192,768]{1,0:T(8,128)(2,1)} %get-tuple-element.176), channel_id=1, source_target_pairs={{0,1},{1,0},{2,3},{3,2},{4,5},{5,4},{6,7},{7,6},{8,9},{9,8},{10,11... | collective-permute-start | bytes 884744 | tf_op jit(solution)/shard_map/ppermute | solution.py:581
  9.8 7.4 %collective-permute-start.2 = (bf16[1,1536]{1,0:T(2,128)(2,1)S(1)}, bf16[1,1536]{1,0:T(2,128)(2,1)S(1)}, u32[]{:S(2)}, u32[]{:S(2)}) collective-permute-start(bf16[1,1536]{1,0:T(2,128)(2,1)S(1)} %reshape.157), channel_id=1, source_target_pairs={{0,1},{1,0},{2,3},{3,2},{4,5},{5,4},{6,7},{7,6},{8,9},{9,8},{10,11... | collective-permute-start | bytes 9224 | tf_op jit(solution)/shard_map/ppermute | solution.py:581
  10.0 7.3 %collective-permute-start.1 = (bf16[8,384]{1,0:T(8,128)(2,1)S(1)}, bf16[8,384]{1,0:T(8,128)(2,1)S(1)}, u32[]{:S(2)}, u32[]{:S(2)}) collective-permute-start(bf16[8,384]{1,0:T(8,128)(2,1)S(1)} %pad_maximum_fusion.2.refs_3_), channel_id=1, source_target_pairs={{0,1},{1,0},{2,3},{3,2},{4,5},{5,4},{6,7},{7,6},{8,9},{9,8},{10,11... | collective-permute-start | bytes 18440 | tf_op jit(solution)/shard_map/ppermute | solution.py:581
  21.2 2.2 collective-permute-start.5
  21.3 11.9 %collective-permute-start.3 = (bf16[192,768]{1,0:T(8,128)(2,1)S(1)}, bf16[192,768]{1,0:T(8,128)(2,1)S(1)}, u32[]{:S(2)}, u32[]{:S(2)}) collective-permute-start(bf16[192,768]{1,0:T(8,128)(2,1)S(1)} %copy-done.43), channel_id=1, source_target_pairs={{0,1},{1,0},{2,3},{3,2},{4,5},{5,4},{6,7},{7,6},{8,9},{9,8},{10,11... | collective-permute-start | bytes 884744 | tf_op jit(solution)/shard_map/ppermute | solution.py:581
  22.5 14.5 %collective-permute-start.4 = (bf16[192,768]{1,0:T(8,128)(2,1)S(1)}, bf16[192,768]{1,0:T(8,128)(2,1)S(1)}, u32[]{:S(2)}, u32[]{:S(2)}) collective-permute-start(bf16[192,768]{1,0:T(8,128)(2,1)S(1)} %copy-done.41), channel_id=1, source_target_pairs={{0,1},{1,0},{2,3},{3,2},{4,5},{5,4},{6,7},{7,6},{8,9},{9,8},{10,11... | collective-permute-start | bytes 884744 | tf_op jit(solution)/shard_map/ppermute | solution.py:581
  33.2 32.0 %copy-start.22 = (bf16[1024,256]{1,0:T(8,128)(2,1)}, bf16[1024,256]{1,0:T(8,128)(2,1)S(1)}, u32[]{:S(2)}) copy-start(bf16[1024,256]{1,0:T(8,128)(2,1)S(1)} %get-tuple-element.210.refs_2_.refs_3_) | copy-start | bytes 1572868
  37.1 2.8 collective-permute-start.7
  37.1 21.4 %collective-permute-start.6 = (bf16[192,768]{1,0:T(8,128)(2,1)S(1)}, bf16[192,768]{1,0:T(8,128)(2,1)S(1)}, u32[]{:S(2)}, u32[]{:S(2)}) collective-permute-start(bf16[192,768]{1,0:T(8,128)(2,1)S(1)} %get-tuple-element.195), channel_id=1, source_target_pairs={{0,1},{1,0},{2,3},{3,2},{4,5},{5,4},{6,7},{7,6},{8,9},{9,8},{10,11... | collective-permute-start | bytes 884744 | tf_op jit(solution)/shard_map/ppermute | solution.py:581
  38.2 1.6 collective-permute-start.8
  49.1 16.1 %copy-start.24 = (bf16[1024,256]{1,0:T(8,128)(2,1)}, bf16[1024,256]{1,0:T(8,128)(2,1)S(1)}, u32[]{:S(2)}) copy-start(bf16[1024,256]{1,0:T(8,128)(2,1)S(1)} %get-tuple-element.211.refs_3_) | copy-start | bytes 1572868
  58.5 6.7 %collective-permute-start.9 = (bf16[1,192,768]{2,1,0:T(8,128)(2,1)S(1)}, bf16[1,192,768]{2,1,0:T(8,128)(2,1)S(1)}, u32[]{:S(2)}, u32[]{:S(2)}) collective-permute-start(bf16[1,192,768]{2,1,0:T(8,128)(2,1)S(1)} %bitcast.57), channel_id=1, source_target_pairs={{0,2},{2,0},{4,6},{6,4},{8,10},{10,8},{12,14},{14,12},{16,18},{18,... | collective-permute-start | bytes 884744 | tf_op jit(solution)/shard_map/ppermute | solution.py:581
  63.0 28.9 %collective-permute-start.10 = (bf16[2,384,768]{2,1,0:T(8,128)(2,1)S(1)}, bf16[2,384,768]{2,1,0:T(8,128)(2,1)S(1)}, u32[]{:S(2)}, u32[]{:S(2)}) collective-permute-start(bf16[2,384,768]{2,1,0:T(8,128)(2,1)S(1)} %pad_maximum_fusion), channel_id=1, source_target_pairs={{0,1},{1,0},{2,3},{3,2},{4,5},{5,4},{6,7},{7,6},{8,9},{9,8},{10,11... | collective-permute-start | bytes 3538952 | tf_op jit(solution)/shard_map/ppermute | solution.py:581
  65.1 51.9 %collective-permute-start.13 = (bf16[2,384,768]{2,1,0:T(8,128)(2,1)S(1)}, bf16[2,384,768]{2,1,0:T(8,128)(2,1)S(1)}, u32[]{:S(2)}, u32[]{:S(2)}) collective-permute-start(bf16[2,384,768]{2,1,0:T(8,128)(2,1)S(1)} %pad_maximum_fusion.1), channel_id=1, source_target_pairs={{0,1},{1,0},{2,3},{3,2},{4,5},{5,4},{6,7},{7,6},{8,9},{9,8},{10,11... | collective-permute-start | bytes 3538952 | tf_op jit(solution)/shard_map/ppermute | solution.py:581
  91.9 9.7 %collective-permute-start.11 = (bf16[1,2,384,768]{3,2,1,0:T(8,128)(2,1)S(1)}, bf16[1,2,384,768]{3,2,1,0:T(8,128)(2,1)S(1)}, u32[]{:S(2)}, u32[]{:S(2)}) collective-permute-start(bf16[1,2,384,768]{3,2,1,0:T(8,128)(2,1)S(1)} %bitcast.67), channel_id=1, source_target_pairs={{0,2},{2,0},{4,6},{6,4},{8,10},{10,8},{12,14},{14,12},{16,18},{18,... | collective-permute-start | bytes 3538952 | tf_op jit(solution)/shard_map/ppermute | solution.py:581
  117.0 2.8 collective-permute-start.14
  117.0 4.5 %collective-permute-start.12 = (bf16[768,768]{1,0:T(8,128)(2,1)S(1)}, bf16[768,768]{1,0:T(8,128)(2,1)S(1)}, u32[]{:S(2)}, u32[]{:S(2)}) collective-permute-start(bf16[768,768]{1,0:T(8,128)(2,1)S(1)} %get-tuple-element.230), channel_id=1, source_target_pairs={{0,2},{2,0},{4,6},{6,4},{8,10},{10,8},{12,14},{14,12},{16,18},{18,... | collective-permute-start | bytes 3538952 | tf_op jit(solution)/shard_map/ppermute | solution.py:581
  121.8 13.9 %collective-permute-start.15 = (bf16[768,768]{1,0:T(8,128)(2,1)}, bf16[768,768]{1,0:T(8,128)(2,1)}, u32[]{:S(2)}, u32[]{:S(2)}) collective-permute-start(bf16[768,768]{1,0:T(8,128)(2,1)} %get-tuple-element.244), channel_id=1, source_target_pairs={{0,2},{2,0},{4,6},{6,4},{8,10},{10,8},{12,14},{14,12},{16,18},{18,... | collective-permute-start | bytes 3538952 | tf_op jit(solution)/shard_map/ppermute | solution.py:581
  122.0 13.7 %collective-permute-start.16 = (bf16[768,768]{1,0:T(8,128)(2,1)}, bf16[768,768]{1,0:T(8,128)(2,1)}, u32[]{:S(2)}, u32[]{:S(2)}) collective-permute-start(bf16[768,768]{1,0:T(8,128)(2,1)} %get-tuple-element.248), channel_id=1, source_target_pairs={{0,2},{2,0},{4,6},{6,4},{8,10},{10,8},{12,14},{14,12},{16,18},{18,... | collective-permute-start | bytes 3538952 | tf_op jit(solution)/shard_map/ppermute | solution.py:581
  133.8 15.3 %collective-permute-start.17 = (bf16[768,768]{1,0:T(8,128)(2,1)}, bf16[768,768]{1,0:T(8,128)(2,1)}, u32[]{:S(2)}, u32[]{:S(2)}) collective-permute-start(bf16[768,768]{1,0:T(8,128)(2,1)} %get-tuple-element.242), channel_id=1, source_target_pairs={{0,2},{2,0},{4,6},{6,4},{8,10},{10,8},{12,14},{14,12},{16,18},{18,... | collective-permute-start | bytes 3538952 | tf_op jit(solution)/shard_map/ppermute | solution.py:581
  134.0 32.4 %collective-permute-start.19 = (bf16[768,768]{1,0:T(8,128)(2,1)S(1)}, bf16[768,768]{1,0:T(8,128)(2,1)S(1)}, u32[]{:S(2)}, u32[]{:S(2)}) collective-permute-start(bf16[768,768]{1,0:T(8,128)(2,1)S(1)} %combine.25), channel_id=1, source_target_pairs={{0,1},{1,0},{2,3},{3,2},{4,5},{5,4},{6,7},{7,6},{8,9},{9,8},{10,11... | collective-permute-start | bytes 3538952 | tf_op jit(solution)/shard_map/ppermute | solution.py:581
  151.5 29.0 %collective-permute-start.18 = (bf16[384,768]{1,0:T(8,128)(2,1)S(1)}, bf16[384,768]{1,0:T(8,128)(2,1)S(1)}, u32[]{:S(2)}, u32[]{:S(2)}) collective-permute-start(bf16[384,768]{1,0:T(8,128)(2,1)S(1)} %get-tuple-element.260), channel_id=1, source_target_pairs={{0,4},{2,6},{4,0},{6,2},{8,12},{10,14},{12,8},{14,10},{16,20},{18,... | collective-permute-start | bytes 1769480 | tf_op jit(solution)/shard_map/ppermute | solution.py:581
  151.7 28.7 %collective-permute-start.20 = (bf16[384,768]{1,0:T(8,128)(2,1)S(1)}, bf16[384,768]{1,0:T(8,128)(2,1)S(1)}, u32[]{:S(2)}, u32[]{:S(2)}) collective-permute-start(bf16[384,768]{1,0:T(8,128)(2,1)S(1)} %get-tuple-element.266), channel_id=1, source_target_pairs={{0,4},{2,6},{4,0},{6,2},{8,12},{10,14},{12,8},{14,10},{16,20},{18,... | collective-permute-start | bytes 1769480 | tf_op jit(solution)/shard_map/ppermute | solution.py:581
  153.6 12.8 %copy-start.15 = (bf16[768,768]{1,0:T(8,128)(2,1)S(1)}, bf16[768,768]{1,0:T(8,128)(2,1)}, u32[]{:S(2)}) copy-start(bf16[768,768]{1,0:T(8,128)(2,1)} %copy-done.14) | copy-start | bytes 3538948
  164.1 20.9 %collective-permute-start.21 = (bf16[2,384,768]{2,1,0:T(8,128)(2,1)S(1)}, bf16[2,384,768]{2,1,0:T(8,128)(2,1)S(1)}, u32[]{:S(2)}, u32[]{:S(2)}) collective-permute-start(bf16[2,384,768]{2,1,0:T(8,128)(2,1)S(1)} %get-tuple-element.272), channel_id=1, source_target_pairs={{0,2},{2,0},{4,6},{6,4},{8,10},{10,8},{12,14},{14,12},{16,18},{18,... | collective-permute-start | bytes 3538952 | tf_op jit(solution)/shard_map/ppermute | solution.py:581
  168.2 34.6 %collective-permute-start.23 = (bf16[384,768]{1,0:T(8,128)(2,1)S(1)}, bf16[384,768]{1,0:T(8,128)(2,1)S(1)}, u32[]{:S(2)}, u32[]{:S(2)}) collective-permute-start(bf16[384,768]{1,0:T(8,128)(2,1)S(1)} %get-tuple-element.276), channel_id=1, source_target_pairs={{0,4},{2,6},{4,0},{6,2},{8,12},{10,14},{12,8},{14,10},{16,20},{18,... | collective-permute-start | bytes 1769480 | tf_op jit(solution)/shard_map/ppermute | solution.py:581
  180.5 18.6 %collective-permute-start.24 = (bf16[384,768]{1,0:T(8,128)(2,1)S(1)}, bf16[384,768]{1,0:T(8,128)(2,1)S(1)}, u32[]{:S(2)}, u32[]{:S(2)}) collective-permute-start(bf16[384,768]{1,0:T(8,128)(2,1)S(1)} %combine.28), channel_id=1, source_target_pairs={{0,1},{1,0},{2,3},{3,2},{4,5},{5,4},{6,7},{7,6},{8,9},{9,8},{10,11... | collective-permute-start | bytes 1769480 | tf_op jit(solution)/shard_map/ppermute | solution.py:581
  185.1 36.3 %collective-permute-start.25 = (bf16[384,768]{1,0:T(8,128)(2,1)S(1)}, bf16[384,768]{1,0:T(8,128)(2,1)S(1)}, u32[]{:S(2)}, u32[]{:S(2)}) collective-permute-start(bf16[384,768]{1,0:T(8,128)(2,1)S(1)} %combine.29), channel_id=1, source_target_pairs={{0,1},{1,0},{2,3},{3,2},{4,5},{5,4},{6,7},{7,6},{8,9},{9,8},{10,11... | collective-permute-start | bytes 1769480 | tf_op jit(solution)/shard_map/ppermute | solution.py:581
  186.6 16.6 %copy-start.34 = (bf16[768,768]{1,0:T(8,128)(2,1)S(1)}, bf16[768,768]{1,0:T(8,128)(2,1)}, u32[]{:S(2)}) copy-start(bf16[768,768]{1,0:T(8,128)(2,1)} %get-tuple-element.301.refs_8_) | copy-start | bytes 3538948
  186.6 16.6 %copy-start.35 = (bf16[768,768]{1,0:T(8,128)(2,1)S(1)}, bf16[768,768]{1,0:T(8,128)(2,1)}, u32[]{:S(2)}) copy-start(bf16[768,768]{1,0:T(8,128)(2,1)} %get-tuple-element.302.refs_9_) | copy-start | bytes 3538948
  186.6 16.6 %copy-start.46 = (bf16[1024,768]{1,0:T(8,128)(2,1)S(1)}, bf16[1024,768]{1,0:T(8,128)(2,1)}, u32[]{:S(2)}) copy-start(bf16[1024,768]{1,0:T(8,128)(2,1)} %get-tuple-element.297.refs_4_) | copy-start | bytes 4718596
  186.6 16.6 %copy-start.47 = (bf16[1024,768]{1,0:T(8,128)(2,1)S(1)}, bf16[1024,768]{1,0:T(8,128)(2,1)}, u32[]{:S(2)}) copy-start(bf16[1024,768]{1,0:T(8,128)(2,1)} %get-tuple-element.298.refs_5_) | copy-start | bytes 4718596
  199.3 21.3 %collective-permute-start.27 = (bf16[192,768]{1,0:T(8,128)(2,1)S(1)}, bf16[192,768]{1,0:T(8,128)(2,1)S(1)}, u32[]{:S(2)}, u32[]{:S(2)}) collective-permute-start(bf16[192,768]{1,0:T(8,128)(2,1)S(1)} %get-tuple-element.294), channel_id=1, source_target_pairs={{0,8},{2,10},{4,12},{6,14},{8,0},{10,2},{12,4},{14,6},{16,24},{18,... | collective-permute-start | bytes 884744 | tf_op jit(solution)/shard_map/ppermute | solution.py:581
  202.9 15.1 %collective-permute-start.26 = (bf16[192,768]{1,0:T(8,128)(2,1)S(1)}, bf16[192,768]{1,0:T(8,128)(2,1)S(1)}, u32[]{:S(2)}, u32[]{:S(2)}) collective-permute-start(bf16[192,768]{1,0:T(8,128)(2,1)S(1)} %get-tuple-element.291), channel_id=1, source_target_pairs={{0,8},{2,10},{4,12},{6,14},{8,0},{10,2},{12,4},{14,6},{16,24},{18,... | collective-permute-start | bytes 884744 | tf_op jit(solution)/shard_map/ppermute | solution.py:581
  203.0 20.6 %collective-permute-start.22 = (bf16[2,384,768]{2,1,0:T(8,128)(2,1)S(1)}, bf16[2,384,768]{2,1,0:T(8,128)(2,1)S(1)}, u32[]{:S(2)}, u32[]{:S(2)}) collective-permute-start(bf16[2,384,768]{2,1,0:T(8,128)(2,1)S(1)} %get-tuple-element.287), channel_id=1, source_target_pairs={{0,2},{2,0},{4,6},{6,4},{8,10},{10,8},{12,14},{14,12},{16,18},{18,... | collective-permute-start | bytes 3538952 | tf_op jit(solution)/shard_map/ppermute | solution.py:581
  204.6 20.2 %copy-start.50 = (bf16[1024,768]{1,0:T(8,128)(2,1)S(1)}, bf16[1024,768]{1,0:T(8,128)(2,1)}, u32[]{:S(2)}) copy-start(bf16[1024,768]{1,0:T(8,128)(2,1)} %get-tuple-element.314.refs_3_) | copy-start | bytes 4718596
  204.6 20.2 %copy-start.51 = (bf16[1024,768]{1,0:T(8,128)(2,1)S(1)}, bf16[1024,768]{1,0:T(8,128)(2,1)}, u32[]{:S(2)}) copy-start(bf16[1024,768]{1,0:T(8,128)(2,1)} %get-tuple-element.315.refs_4_) | copy-start | bytes 4718596
  204.6 20.2 %copy-start.52 = (bf16[1024,768]{1,0:T(8,128)(2,1)S(1)}, bf16[1024,768]{1,0:T(8,128)(2,1)}, u32[]{:S(2)}) copy-start(bf16[1024,768]{1,0:T(8,128)(2,1)} %get-tuple-element.316.refs_5_) | copy-start | bytes 4718596
  204.6 20.2 %copy-start.53 = (bf16[768,768]{1,0:T(8,128)(2,1)S(1)}, bf16[768,768]{1,0:T(8,128)(2,1)}, u32[]{:S(2)}) copy-start(bf16[768,768]{1,0:T(8,128)(2,1)} %get-tuple-element.317.refs_8_) | copy-start | bytes 3538948
  204.6 20.2 %copy-start.54 = (bf16[768,768]{1,0:T(8,128)(2,1)S(1)}, bf16[768,768]{1,0:T(8,128)(2,1)}, u32[]{:S(2)}) copy-start(bf16[768,768]{1,0:T(8,128)(2,1)} %get-tuple-element.318.refs_9_) | copy-start | bytes 3538948
  215.8 5.5 %collective-permute-start.28 = (f32[12,384]{1,0:T(8,128)S(1)}, f32[12,384]{1,0:T(8,128)S(1)}, u32[]{:S(2)}, u32[]{:S(2)}) collective-permute-start(f32[12,384]{1,0:T(8,128)S(1)} %get-tuple-element.352), channel_id=1, source_target_pairs={{0,1},{1,0},{2,3},{3,2},{4,5},{5,4},{6,7},{7,6},{8,9},{9,8},{10,11... | collective-permute-start | bytes 55304 | tf_op jit(solution)/shard_map/ppermute | solution.py:581
  218.1 23.5 %collective-permute-start.32 = (bf16[192,768]{1,0:T(8,128)(2,1)S(1)}, bf16[192,768]{1,0:T(8,128)(2,1)S(1)}, u32[]{:S(2)}, u32[]{:S(2)}) collective-permute-start(bf16[192,768]{1,0:T(8,128)(2,1)S(1)} %combine.34.refs_0_), channel_id=1, source_target_pairs={{0,16},{2,18},{4,20},{6,22},{8,24},{10,26},{12,28},{14,30},{16,0},... | collective-permute-start | bytes 884744 | tf_op jit(solution)/shard_map/ppermute | solution.py:581
  220.7 26.5 %collective-permute-start.37 = (bf16[192,768]{1,0:T(8,128)(2,1)S(1)}, bf16[192,768]{1,0:T(8,128)(2,1)S(1)}, u32[]{:S(2)}, u32[]{:S(2)}) collective-permute-start(bf16[192,768]{1,0:T(8,128)(2,1)S(1)} %combine.35.refs_0_), channel_id=1, source_target_pairs={{0,16},{2,18},{4,20},{6,22},{8,24},{10,26},{12,28},{14,30},{16,0},... | collective-permute-start | bytes 884744 | tf_op jit(solution)/shard_map/ppermute | solution.py:581
  221.3 16.0 %collective-permute-start.29 = (f32[12,384]{1,0:T(8,128)S(1)}, f32[12,384]{1,0:T(8,128)S(1)}, u32[]{:S(2)}, u32[]{:S(2)}) collective-permute-start(f32[12,384]{1,0:T(8,128)S(1)} %combine.36.refs_0_), channel_id=1, source_target_pairs={{0,4},{2,6},{4,0},{6,2},{8,12},{10,14},{12,8},{14,10},{16,20},{18,... | collective-permute-start | bytes 55304 | tf_op jit(solution)/shard_map/ppermute | solution.py:581
  221.6 20.1 %collective-permute-start.31 = (bf16[192,768]{1,0:T(8,128)(2,1)S(1)}, bf16[192,768]{1,0:T(8,128)(2,1)S(1)}, u32[]{:S(2)}, u32[]{:S(2)}) collective-permute-start(bf16[192,768]{1,0:T(8,128)(2,1)S(1)} %get-tuple-element.307), channel_id=1, source_target_pairs={{0,4},{2,6},{4,0},{6,2},{8,12},{10,14},{12,8},{14,10},{16,20},{18,... | collective-permute-start | bytes 884744 | tf_op jit(solution)/shard_map/ppermute | solution.py:581
  223.8 18.0 %collective-permute-start.34 = (bf16[384,768]{1,0:T(8,128)(2,1)S(1)}, bf16[384,768]{1,0:T(8,128)(2,1)S(1)}, u32[]{:S(2)}, u32[]{:S(2)}) collective-permute-start(bf16[384,768]{1,0:T(8,128)(2,1)S(1)} %combine.32), channel_id=1, source_target_pairs={{0,1},{1,0},{2,3},{3,2},{4,5},{5,4},{6,7},{7,6},{8,9},{9,8},{10,11... | collective-permute-start | bytes 1769480 | tf_op jit(solution)/shard_map/ppermute | solution.py:581
  241.7 11.9 %collective-permute-start.36 = (bf16[192,768]{1,0:T(8,128)(2,1)S(1)}, bf16[192,768]{1,0:T(8,128)(2,1)S(1)}, u32[]{:S(2)}, u32[]{:S(2)}) collective-permute-start(bf16[192,768]{1,0:T(8,128)(2,1)S(1)} %combine.38.part_ref), channel_id=1, source_target_pairs={{0,8},{2,10},{4,12},{6,14},{8,0},{10,2},{12,4},{14,6},{16,24},{18,... | collective-permute-start | bytes 884744 | tf_op jit(solution)/shard_map/ppermute | solution.py:581
  242.1 11.8 %collective-permute-start.35 = (bf16[192,768]{1,0:T(8,128)(2,1)S(1)}, bf16[192,768]{1,0:T(8,128)(2,1)S(1)}, u32[]{:S(2)}, u32[]{:S(2)}) collective-permute-start(bf16[192,768]{1,0:T(8,128)(2,1)S(1)} %get-tuple-element.325), channel_id=1, source_target_pairs={{0,4},{2,6},{4,0},{6,2},{8,12},{10,14},{12,8},{14,10},{16,20},{18,... | collective-permute-start | bytes 884744 | tf_op jit(solution)/shard_map/ppermute | solution.py:581
  242.4 17.5 %collective-permute-start.33 = (bf16[192,768]{1,0:T(8,128)(2,1)S(1)}, bf16[192,768]{1,0:T(8,128)(2,1)S(1)}, u32[]{:S(2)}, u32[]{:S(2)}) collective-permute-start(bf16[192,768]{1,0:T(8,128)(2,1)S(1)} %combine.39.refs_0_), channel_id=1, source_target_pairs={{0,8},{2,10},{4,12},{6,14},{8,0},{10,2},{12,4},{14,6},{16,24},{18,... | collective-permute-start | bytes 884744 | tf_op jit(solution)/shard_map/ppermute | solution.py:581
  247.3 20.5 %collective-permute-start.43 = (bf16[192,768]{1,0:T(8,128)(2,1)S(1)}, bf16[192,768]{1,0:T(8,128)(2,1)S(1)}, u32[]{:S(2)}, u32[]{:S(2)}) collective-permute-start(bf16[192,768]{1,0:T(8,128)(2,1)S(1)} %combine.41.part_ref), channel_id=1, source_target_pairs={{0,8},{2,10},{4,12},{6,14},{8,0},{10,2},{12,4},{14,6},{16,24},{18,... | collective-permute-start | bytes 884744 | tf_op jit(solution)/shard_map/ppermute | solution.py:581
  253.6 27.1 %collective-permute-start.41 = (bf16[384,768]{1,0:T(8,128)(2,1)S(1)}, bf16[384,768]{1,0:T(8,128)(2,1)S(1)}, u32[]{:S(2)}, u32[]{:S(2)}) collective-permute-start(bf16[384,768]{1,0:T(8,128)(2,1)S(1)} %join.6.part_ref), channel_id=1, source_target_pairs={{0,4},{2,6},{4,0},{6,2},{8,12},{10,14},{12,8},{14,10},{16,20},{18,... | collective-permute-start | bytes 1769480 | tf_op jit(solution)/shard_map/ppermute | solution.py:581
  253.9 12.8 %collective-permute-start.30 = (f32[12,384]{1,0:T(8,128)S(1)}, f32[12,384]{1,0:T(8,128)S(1)}, u32[]{:S(2)}, u32[]{:S(2)}) collective-permute-start(f32[12,384]{1,0:T(8,128)S(1)} %combine.37.refs_0_), channel_id=1, source_target_pairs={{0,8},{2,10},{4,12},{6,14},{8,0},{10,2},{12,4},{14,6},{16,24},{18,... | collective-permute-start | bytes 55304 | tf_op jit(solution)/shard_map/ppermute | solution.py:581
  266.7 1.2 collective-permute-start.38
  266.7 13.9 %collective-permute-start.42 = (bf16[192,768]{1,0:T(8,128)(2,1)S(1)}, bf16[192,768]{1,0:T(8,128)(2,1)S(1)}, u32[]{:S(2)}, u32[]{:S(2)}) collective-permute-start(bf16[192,768]{1,0:T(8,128)(2,1)S(1)} %combine.42.refs_0_), channel_id=1, source_target_pairs={{0,8},{2,10},{4,12},{6,14},{8,0},{10,2},{12,4},{14,6},{16,24},{18,... | collective-permute-start | bytes 884744 | tf_op jit(solution)/shard_map/ppermute | solution.py:581
  267.9 30.5 %collective-permute-start.45 = (bf16[384,768]{1,0:T(8,128)(2,1)S(1)}, bf16[384,768]{1,0:T(8,128)(2,1)S(1)}, u32[]{:S(2)}, u32[]{:S(2)}) collective-permute-start(bf16[384,768]{1,0:T(8,128)(2,1)S(1)} %join.7.part_ref), channel_id=1, source_target_pairs={{0,4},{2,6},{4,0},{6,2},{8,12},{10,14},{12,8},{14,10},{16,20},{18,... | collective-permute-start | bytes 1769480 | tf_op jit(solution)/shard_map/ppermute | solution.py:581
  268.2 23.4 %collective-permute-start.40 = (bf16[192,768]{1,0:T(8,128)(2,1)S(1)}, bf16[192,768]{1,0:T(8,128)(2,1)S(1)}, u32[]{:S(2)}, u32[]{:S(2)}) collective-permute-start(bf16[192,768]{1,0:T(8,128)(2,1)S(1)} %combine.43.refs_0_), channel_id=1, source_target_pairs={{0,16},{2,18},{4,20},{6,22},{8,24},{10,26},{12,28},{14,30},{16,0},... | collective-permute-start | bytes 884744 | tf_op jit(solution)/shard_map/ppermute | solution.py:581
  280.7 17.7 %collective-permute-start.46 = (bf16[192,768]{1,0:T(8,128)(2,1)S(1)}, bf16[192,768]{1,0:T(8,128)(2,1)S(1)}, u32[]{:S(2)}, u32[]{:S(2)}) collective-permute-start(bf16[192,768]{1,0:T(8,128)(2,1)S(1)} %combine.46.refs_0_), channel_id=1, source_target_pairs={{0,16},{2,18},{4,20},{6,22},{8,24},{10,26},{12,28},{14,30},{16,0},... | collective-permute-start | bytes 884744 | tf_op jit(solution)/shard_map/ppermute | solution.py:581
  291.7 7.3 %collective-permute-start.44 = (bf16[192,768]{1,0:T(8,128)(2,1)S(1)}, bf16[192,768]{1,0:T(8,128)(2,1)S(1)}, u32[]{:S(2)}, u32[]{:S(2)}) collective-permute-start(bf16[192,768]{1,0:T(8,128)(2,1)S(1)} %combine.47.part_ref), channel_id=1, source_target_pairs={{0,4},{2,6},{4,0},{6,2},{8,12},{10,14},{12,8},{14,10},{16,20},{18,... | collective-permute-start | bytes 884744 | tf_op jit(solution)/shard_map/ppermute | solution.py:581
  293.6 4.7 %collective-permute-start.39 = (f32[12,384]{1,0:T(8,128)S(1)}, f32[12,384]{1,0:T(8,128)S(1)}, u32[]{:S(2)}, u32[]{:S(2)}) collective-permute-start(f32[12,384]{1,0:T(8,128)S(1)} %combine.45.refs_0_), channel_id=1, source_target_pairs={{0,16},{2,18},{4,20},{6,22},{8,24},{10,26},{12,28},{14,30},{16,0},... | collective-permute-start | bytes 55304 | tf_op jit(solution)/shard_map/ppermute | solution.py:581
  299.0 10.7 %collective-permute-start.47 = (bf16[384,768]{1,0:T(8,128)(2,1)S(1)}, bf16[384,768]{1,0:T(8,128)(2,1)}, u32[]{:S(2)}, u32[]{:S(2)}) collective-permute-start(bf16[384,768]{1,0:T(8,128)(2,1)S(1)} %join.10), channel_id=1, source_target_pairs={{0,2},{2,0},{4,6},{6,4},{8,10},{10,8},{12,14},{14,12},{16,18},{18,... | collective-permute-start | bytes 1769480 | tf_op jit(solution)/shard_map/ppermute | solution.py:581
  299.1 9.5 %collective-permute-start.48 = (bf16[192,768]{1,0:T(8,128)(2,1)S(1)}, bf16[192,768]{1,0:T(8,128)(2,1)}, u32[]{:S(2)}, u32[]{:S(2)}) collective-permute-start(bf16[192,768]{1,0:T(8,128)(2,1)S(1)} %combine.49.part_ref), channel_id=1, source_target_pairs={{0,4},{2,6},{4,0},{6,2},{8,12},{10,14},{12,8},{14,10},{16,20},{18,... | collective-permute-start | bytes 884744 | tf_op jit(solution)/shard_map/ppermute | solution.py:581
  300.7 13.8 %collective-permute-start.50 = (bf16[768,768]{1,0:T(8,128)(2,1)S(1)}, bf16[768,768]{1,0:T(8,128)(2,1)}, u32[]{:S(2)}, u32[]{:S(2)}) collective-permute-start(bf16[768,768]{1,0:T(8,128)(2,1)S(1)} %join.8), channel_id=1, source_target_pairs={{0,2},{2,0},{4,6},{6,4},{8,10},{10,8},{12,14},{14,12},{16,18},{18,... | collective-permute-start | bytes 3538952 | tf_op jit(solution)/shard_map/ppermute | solution.py:581
  302.1 13.8 %collective-permute-start.51 = (bf16[768,768]{1,0:T(8,128)(2,1)S(1)}, bf16[768,768]{1,0:T(8,128)(2,1)S(1)}, u32[]{:S(2)}, u32[]{:S(2)}) collective-permute-start(bf16[768,768]{1,0:T(8,128)(2,1)S(1)} %join.9), channel_id=1, source_target_pairs={{0,2},{2,0},{4,6},{6,4},{8,10},{10,8},{12,14},{14,12},{16,18},{18,... | collective-permute-start | bytes 3538952 | tf_op jit(solution)/shard_map/ppermute | solution.py:581
  309.7 2.4 collective-permute-start.49
  (48 other events, 181.7 us)
